TPU v7x, 256 devices: a whole 4x4x8 slice. The times are simulated.
256 devices in a mesh: ops: 4 (over y), blk: 64 (over x, z, core).
Axes of the slice: x: 4, y: 4, z: 8, core: 2. Of those that a mesh axis runs over, the one named last changes fastest.
Arguments:
- psi: bfloat16 [16384, 8192], P('blk'), may hold values from -6 to 6
- left_env: bfloat16 [16, 64, 256, 256], P('ops', 'blk'), may hold values from -0.09375 to 0.09375
- right_env: bfloat16 [16, 64, 128, 128], P('ops', 'blk'), may hold values from -0.5 to 0.5
- left_live: int32 [64], replicated, may hold values from 64 to 256, as said below
- right_live: int32 [64], replicated, may hold values from 32 to 128, as said below
Outputs:
- hpsi: float32 [16384, 8192], P('blk', 'ops')
Inputs may be any that keep to these rules, and one draw needn't show every extreme that they name: `left_live`: some left sector is fully live. `right_live`: some right sector is fully live.
All inputs are finite; a program needn't handle non-finite values.
Results may differ from a plain program's by a relative error of at most 0.0029.
Values may be sent and summed in bfloat16 or wider, within the bound.
No kernel may reach another device: no remote copies, remote signals or barrier semaphores. Data moves between devices by JAX's collectives and lax.ppermute only.
A program may use at most 128 MiB of HBM per device.

v0:
```python
import functools

import jax
import jax.numpy as jnp
from jax import lax
from jax.experimental import pallas as pl
from jax.experimental.pallas import tpu as pltpu
from jax.sharding import PartitionSpec as P


X, Y, Z, C = 4, 4, 8, 2
AXES = ("ops", "blk")


def device(x, y, z, c):
    return (y % Y) * (X * Z * C) + (x % X) * (Z * C) + (z % Z) * C + (c % C)


def permute(value, move):
    pairs = []
    for y in range(Y):
        for x in range(X):
            for z in range(Z):
                for c in range(C):
                    pairs.append((device(x, y, z, c), device(*move(x, y, z, c))))
    return lax.ppermute(value, AXES, pairs)


def spread(k):
    return lambda x, y, z, c: (2 * x - y + k, x, z, c)


def along_y(d):
    return lambda x, y, z, c: (x, y - d * (1 - 2 * c), z, c)


def along_z(d):
    return lambda x, y, z, c: (x, y, z + d * (1 - 2 * c), c)


def swap_core(x, y, z, c):
    return (x, y, z, 1 - c)


def place(pos, e):
    z = ((pos[1] >> 1) + e * (2 * (pos[1] & 1) - 1)) & (Z - 1)
    return pos[0] * Z + z, z


def mix(d, size, left, masked_ref, out_ref):
    terms = left.shape[0]
    width = C * size
    for i in range(masked_ref.shape[1] // width):
        value = masked_ref[:, i * width : (i + 1) * width]
        for t in range(terms):
            m = jnp.dot(left[t], value, preferred_element_type=jnp.float32).astype(jnp.bfloat16)
            for p in range(C):
                out_ref[d, i * C + p, :, t * size : (t + 1) * size] = m[:, p * size : (p + 1) * size]


def first_kernel(size, pos, left_live, right_live, psi_ref, left, out_ref, masked_ref):
    rows, span = psi_ref.shape
    col = lax.broadcasted_iota(jnp.int32, (rows, size), 1)
    row_mask = lax.broadcasted_iota(jnp.int32, (rows, size), 0) < left_live[pos[1]]
    for j in range(span // size):
        at = slice(j * size, (j + 1) * size)
        mask = row_mask & (col < right_live[pos[0] * (Z * C) + j])
        value = psi_ref[:, at]
        masked_ref[:, at] = jnp.where(mask, value, jnp.zeros_like(value))
    mix(0, size, left, masked_ref, out_ref)


def next_kernel(d, size, masked_ref, left, kept, out_ref):
    mix(d, size, left, masked_ref, out_ref)


def cost(terms, rows, columns):
    flops = 2 * terms * rows * rows * columns
    return pl.CostEstimate(flops=flops, bytes_accessed=6 << 20, transcendentals=0)


def first_step(scalars, psi, left, size):
    rows = psi.shape[0]
    terms = left.shape[0]
    span = Z * C * size
    vmem = pl.BlockSpec(memory_space=pltpu.VMEM)
    return pl.pallas_call(
        functools.partial(first_kernel, size),
        grid_spec=pltpu.PrefetchScalarGridSpec(
            num_scalar_prefetch=3,
            grid=(1,),
            in_specs=[pl.BlockSpec((rows, span), lambda i, *s: (0, s[0][0])), vmem],
            out_specs=[vmem, vmem],
        ),
        out_shape=[
            jax.ShapeDtypeStruct((Y, Z * C, rows, terms * size), jnp.bfloat16),
            jax.ShapeDtypeStruct((rows, span), jnp.bfloat16),
        ],
        cost_estimate=cost(terms, rows, span),
        compiler_params=pltpu.CompilerParams(vmem_limit_bytes=8 << 20),
        name="mixed",
    )(*scalars, psi, left)


def next_step(d, masked, left, size, mixed):
    vmem = pl.BlockSpec(memory_space=pltpu.VMEM)
    return pl.pallas_call(
        functools.partial(next_kernel, d, size),
        in_specs=[vmem, vmem, vmem],
        out_specs=vmem,
        out_shape=jax.ShapeDtypeStruct(mixed.shape, mixed.dtype),
        input_output_aliases={2: 0},
        cost_estimate=cost(left.shape[0], *masked.shape),
        compiler_params=pltpu.CompilerParams(vmem_limit_bytes=8 << 20),
        name="mixed",
    )(masked, left, mixed)


def pick(values, i):
    out = values[0]
    for n, v in enumerate(values[1:], 1):
        out = jnp.where(i == n, v, out)
    return out


def total_kernel(steps, pos, left_live, right_live, mixed, *rest):
    out_ref = rest[-1]
    rows, width = out_ref.shape
    half = width // C
    y, blk = pos[0], pos[1]
    x, core = blk >> 4, blk & 1
    i = pl.program_id(0)
    there, z = place(pos, pick(steps, i))
    col = lax.broadcasted_iota(jnp.int32, (rows, half), 1)
    row = lax.broadcasted_iota(jnp.int32, (rows, half), 0)
    row_mask = row < left_live[blk]

    def one(oa, ob, pa, pb):
        for which, parts in ((core, (oa, ob)), (1 - core, (pa, pb))):
            total = None
            for k in range(X):
                ref = parts[k // 2]
                terms = ref.shape[0] // 2
                at = (k % 2) * terms
                rcat = jnp.concatenate([ref[at + t] for t in range(terms)], axis=1)
                part = lax.dot_general(
                    mixed[((y - x + k) * (1 - 2 * core)) & (Y - 1), z * C + which],
                    rcat,
                    (((1,), (1,)), ((), ())),
                    preferred_element_type=jnp.float32,
                )
                total = part if total is None else total + part
            mask = row_mask & (col < right_live[there * C + which])
            lanes = pl.ds(pl.multiple_of(which * half, half), half)
            out_ref[:, lanes] = jnp.where(mask, total, jnp.zeros_like(total))

    for n in range(len(steps)):
        pl.when(i == n)(functools.partial(one, *rest[4 * n : 4 * n + 4]))


def total_step(steps, scalars, mixed, rights, out):
    groups, _, rows, depth = mixed.shape
    size = rights[0].shape[1]
    width = C * size
    columns = Z * width
    in_specs = [pl.BlockSpec(memory_space=pltpu.VMEM)] * (1 + len(rights))
    args = [*scalars, mixed, *rights]
    aliases = {}
    if out is not None:
        in_specs.append(pl.BlockSpec(memory_space=pl.ANY))
        args.append(out)
        aliases = {len(args) - 1: 0}
    flops = 2 * groups * depth * rows * width * len(steps)
    return pl.pallas_call(
        functools.partial(total_kernel, steps),
        grid_spec=pltpu.PrefetchScalarGridSpec(
            num_scalar_prefetch=3,
            grid=(len(steps),),
            in_specs=in_specs,
            out_specs=pl.BlockSpec(
                (rows, width), lambda i, *s: (0, place(s[0], pick(steps, i))[1])
            ),
        ),
        out_shape=jax.ShapeDtypeStruct((rows, columns), jnp.float32),
        input_output_aliases=aliases,
        cost_estimate=pl.CostEstimate(flops=flops, bytes_accessed=4 << 20, transcendentals=0),
        compiler_params=pltpu.CompilerParams(vmem_limit_bytes=8 << 20),
        name="total",
    )(*args)


def body(psi, left_env, right_env, left_live, right_live):
    pos = jnp.stack([lax.axis_index("ops"), lax.axis_index("blk")]).astype(jnp.int32)
    scalars = (pos, left_live, right_live)
    terms, _, size, _ = right_env.shape
    psi = pltpu.with_memory_space_constraint(psi, pltpu.HBM)
    rank = left_env.shape[2]
    mine = right_env.reshape(terms, size, size)
    left = left_env.reshape(terms, rank, rank)

    groups = [permute(mine, spread(k)) for k in range(X)]
    lefts = {0: left, 1: permute(left, along_y(1)), 3: permute(left, along_y(-1))}
    lefts[2] = permute(lefts[1], along_y(1))

    a = {0: jnp.concatenate(groups[:2], axis=0)}
    b = {0: jnp.concatenate(groups[2:], axis=0)}
    for r in (1, 2, 3):
        for chain in (a, b):
            chain[r] = permute(chain[r - 1], along_z(1))
            chain[-r] = permute(chain[1 - r], along_z(-1))
    a[4] = permute(a[3], along_z(1))
    b[4] = permute(b[-3], along_z(-1))

    mixed, masked = first_step(scalars, psi, left, size)
    for d in (1, 3, 2):
        mixed = next_step(d, masked, lefts[d], size, mixed)
    out = None
    for steps in ((0, 1, -1), (2, -2), (3, -3), (4,)):
        rights = []
        for e in steps:
            twin = e if e in (0, 4) else -e
            rights += [a[e], b[e]]
            rights += [permute(v[twin], swap_core) for v in (a, b)]
        out = total_step(steps, scalars, mixed, rights, out)
    return out


def solution(mesh):
    in_specs = (P("blk", None), P("ops", "blk", None, None), P("ops", "blk", None, None), P(), P())
    out_specs = P("blk", "ops")
    return jax.shard_map(body, mesh=mesh, in_specs=in_specs, out_specs=out_specs, check_vma=False)
```

profile of v0, /device:TPU:1, one launch (start us, length us, event | category | flops | bytes accessed | tf_op | source)
XLA Modules:
  0.0 97.6 jit_solution(4139253796134388664)
XLA Ops:
  0.0 1.6 %collective-permute-start.3 = (bf16[4,128,128]{2,1,0:T(8,128)(2,1)}, bf16[4,128,128]{2,1,0:T(8,128)(2,1)S(1)}, u32[]{:S(2)}, u32[]{:S(2)}) collective-permute-start(bf16[4,128,128]{2,1,0:T(8,128)(2,1)} %bitcast.7), channel_id=1, source_target_pairs={{0,0},{1,1},{2,2},{3,3},{4,4},{5,5},{6,6},{7,7},{8,8},{9,9},{10,10... | collective-permute-start | bytes 393224 | tf_op jit(solution)/shard_map/ppermute | solution.py:26
  1.6 4.7 %collective-permute-start.4 = (bf16[4,128,128]{2,1,0:T(8,128)(2,1)}, bf16[4,128,128]{2,1,0:T(8,128)(2,1)S(1)}, u32[]{:S(2)}, u32[]{:S(2)}) collective-permute-start(bf16[4,128,128]{2,1,0:T(8,128)(2,1)} %bitcast.8), channel_id=1, source_target_pairs={{0,16},{1,17},{2,18},{3,19},{4,20},{5,21},{6,22},{7,23},{8,24},{9,... | collective-permute-start | bytes 393224 | tf_op jit(solution)/shard_map/ppermute | solution.py:26
  6.2 2.3 %collective-permute-start.9 = (bf16[4,128,128]{2,1,0:T(8,128)(2,1)}, bf16[4,128,128]{2,1,0:T(8,128)(2,1)S(1)}, u32[]{:S(2)}, u32[]{:S(2)}) collective-permute-start(bf16[4,128,128]{2,1,0:T(8,128)(2,1)} %bitcast.9), channel_id=1, source_target_pairs={{0,32},{1,33},{2,34},{3,35},{4,36},{5,37},{6,38},{7,39},{8,40},{9,... | collective-permute-start | bytes 393224 | tf_op jit(solution)/shard_map/ppermute | solution.py:26
  8.6 4.6 %collective-permute-start.10 = (bf16[4,128,128]{2,1,0:T(8,128)(2,1)}, bf16[4,128,128]{2,1,0:T(8,128)(2,1)S(1)}, u32[]{:S(2)}, u32[]{:S(2)}) collective-permute-start(bf16[4,128,128]{2,1,0:T(8,128)(2,1)} %bitcast.10), channel_id=1, source_target_pairs={{0,48},{1,49},{2,50},{3,51},{4,52},{5,53},{6,54},{7,55},{8,56},{9,... | collective-permute-start | bytes 393224 | tf_op jit(solution)/shard_map/ppermute | solution.py:26
  13.2 1.7 %collective-permute-start.20 = (bf16[8,128,128]{2,1,0:T(8,128)(2,1)S(1)}, bf16[8,128,128]{2,1,0:T(8,128)(2,1)S(1)}, u32[]{:S(2)}, u32[]{:S(2)}) collective-permute-start(bf16[8,128,128]{2,1,0:T(8,128)(2,1)S(1)} %constant_dynamic-update-slice_fusion.rest_0_), channel_id=1, source_target_pairs={{0,14},{1,3},{2,0},{3,5},{4,2},{5,7},{6,4},{7,9},{8,6},{9,11},{10,... | collective-permute-start | bytes 786440 | tf_op jit(solution)/shard_map/ppermute | solution.py:26
  15.0 2.9 %collective-permute-done.10 = bf16[4,128,128]{2,1,0:T(8,128)(2,1)S(1)} collective-permute-done((bf16[4,128,128]{2,1,0:T(8,128)(2,1)}, bf16[4,128,128]{2,1,0:T(8,128)(2,1)S(1)}, u32[]{:S(2)}, u32[]{:S(2)}) %collective-permute-start.10) | collective-permute-done | bytes 131104 | tf_op jit(solution)/shard_map/ppermute | solution.py:26
  17.9 1.7 %collective-permute-start.11 = (bf16[8,128,128]{2,1,0:T(8,128)(2,1)S(1)}, bf16[8,128,128]{2,1,0:T(8,128)(2,1)S(1)}, u32[]{:S(2)}, u32[]{:S(2)}) collective-permute-start(bf16[8,128,128]{2,1,0:T(8,128)(2,1)S(1)} %constant_dynamic-update-slice_fusion.2.rest_1_), channel_id=1, source_target_pairs={{0,14},{1,3},{2,0},{3,5},{4,2},{5,7},{6,4},{7,9},{8,6},{9,11},{10,... | collective-permute-start | bytes 786440 | tf_op jit(solution)/shard_map/ppermute | solution.py:26
  19.6 4.0 %collective-permute-start.5 = (bf16[8,128,128]{2,1,0:T(8,128)(2,1)S(1)}, bf16[8,128,128]{2,1,0:T(8,128)(2,1)S(1)}, u32[]{:S(2)}, u32[]{:S(2)}) collective-permute-start(bf16[8,128,128]{2,1,0:T(8,128)(2,1)S(1)} %constant_dynamic-update-slice_fusion.rest_0_), channel_id=1, source_target_pairs={{0,2},{1,15},{2,4},{3,1},{4,6},{5,3},{6,8},{7,5},{8,10},{9,7},{10,... | collective-permute-start | bytes 786440 | tf_op jit(solution)/shard_map/ppermute | solution.py:26
  23.7 2.9 %collective-permute-start.2 = (bf16[4,256,256]{2,1,0:T(8,128)(2,1)}, bf16[4,256,256]{2,1,0:T(8,128)(2,1)S(1)}, u32[]{:S(2)}, u32[]{:S(2)}) collective-permute-start(bf16[4,256,256]{2,1,0:T(8,128)(2,1)} %bitcast.5), channel_id=1, source_target_pairs={{0,64},{1,193},{2,66},{3,195},{4,68},{5,197},{6,70},{7,199},{8,72}... | collective-permute-start | bytes 1572872 | tf_op jit(solution)/shard_map/ppermute | solution.py:26
  26.6 1.4 %collective-permute-start.17 = (bf16[8,128,128]{2,1,0:T(8,128)(2,1)S(1)}, bf16[8,128,128]{2,1,0:T(8,128)(2,1)S(1)}, u32[]{:S(2)}, u32[]{:S(2)}) collective-permute-start(bf16[8,128,128]{2,1,0:T(8,128)(2,1)S(1)} %constant_dynamic-update-slice_fusion.2.rest_1_), channel_id=1, source_target_pairs={{0,2},{1,15},{2,4},{3,1},{4,6},{5,3},{6,8},{7,5},{8,10},{9,7},{10,... | collective-permute-start | bytes 786440 | tf_op jit(solution)/shard_map/ppermute | solution.py:26
  27.9 3.4 %collective-permute-start.31 = (bf16[8,128,128]{2,1,0:T(8,128)(2,1)S(1)}, bf16[8,128,128]{2,1,0:T(8,128)(2,1)S(1)}, u32[]{:S(2)}, u32[]{:S(2)}) collective-permute-start(bf16[8,128,128]{2,1,0:T(8,128)(2,1)S(1)} %constant_dynamic-update-slice_fusion.rest_0_), channel_id=1, source_target_pairs={{0,1},{1,0},{2,3},{3,2},{4,5},{5,4},{6,7},{7,6},{8,9},{9,8},{10,11... | collective-permute-start | bytes 786440 | tf_op jit(solution)/shard_map/ppermute | solution.py:26
  31.3 0.9 collective-permute-start.32
  32.2 0.7 collective-permute-done.17.rest_5_
  32.9 4.0 %collective-permute-start.33 = (bf16[8,128,128]{2,1,0:T(8,128)(2,1)S(1)}, bf16[8,128,128]{2,1,0:T(8,128)(2,1)S(1)}, u32[]{:S(2)}, u32[]{:S(2)}) collective-permute-start(bf16[8,128,128]{2,1,0:T(8,128)(2,1)S(1)} %collective-permute-done.20.rest_8_), channel_id=1, source_target_pairs={{0,1},{1,0},{2,3},{3,2},{4,5},{5,4},{6,7},{7,6},{8,9},{9,8},{10,11... | collective-permute-start | bytes 786440 | tf_op jit(solution)/shard_map/ppermute | solution.py:26
  36.9 0.7 copy-done.1
  37.6 0.5 collective-permute-start.35
  38.2 0.7 copy-done.3
  38.9 2.7 %collective-permute-start.6 = (bf16[8,128,128]{2,1,0:T(8,128)(2,1)S(1)}, bf16[8,128,128]{2,1,0:T(8,128)(2,1)}, u32[]{:S(2)}, u32[]{:S(2)}) collective-permute-start(bf16[8,128,128]{2,1,0:T(8,128)(2,1)S(1)} %collective-permute-done.5.rest_4_), channel_id=1, source_target_pairs={{0,2},{1,15},{2,4},{3,1},{4,6},{5,3},{6,8},{7,5},{8,10},{9,7},{10,... | collective-permute-start | bytes 786440 | tf_op jit(solution)/shard_map/ppermute | solution.py:26
  41.6 0.7 copy-done.5
  42.3 1.4 %collective-permute-start.18 = (bf16[8,128,128]{2,1,0:T(8,128)(2,1)S(1)}, bf16[8,128,128]{2,1,0:T(8,128)(2,1)}, u32[]{:S(2)}, u32[]{:S(2)}) collective-permute-start(bf16[8,128,128]{2,1,0:T(8,128)(2,1)S(1)} %collective-permute-done.17.rest_5_), channel_id=1, source_target_pairs={{0,2},{1,15},{2,4},{3,1},{4,6},{5,3},{6,8},{7,5},{8,10},{9,7},{10,... | collective-permute-start | bytes 786440 | tf_op jit(solution)/shard_map/ppermute | solution.py:26
  43.7 0.7 copy-done.7
  44.4 0.9 collective-permute-start.36
  45.3 3.0 %collective-permute-start.27 = (bf16[8,128,128]{2,1,0:T(8,128)(2,1)}, bf16[8,128,128]{2,1,0:T(8,128)(2,1)S(1)}, u32[]{:S(2)}, u32[]{:S(2)}) collective-permute-start(bf16[8,128,128]{2,1,0:T(8,128)(2,1)} %collective-permute-done.21.rest_4_), channel_id=1, source_target_pairs={{0,1},{1,0},{2,3},{3,2},{4,5},{5,4},{6,7},{7,6},{8,9},{9,8},{10,11... | collective-permute-start | bytes 786440 | tf_op jit(solution)/shard_map/ppermute | solution.py:26
  48.3 5.1 %collective-permute-start.28 = (bf16[8,128,128]{2,1,0:T(8,128)(2,1)}, bf16[8,128,128]{2,1,0:T(8,128)(2,1)S(1)}, u32[]{:S(2)}, u32[]{:S(2)}) collective-permute-start(bf16[8,128,128]{2,1,0:T(8,128)(2,1)} %collective-permute-done.12.rest_5_), channel_id=1, source_target_pairs={{0,1},{1,0},{2,3},{3,2},{4,5},{5,4},{6,7},{7,6},{8,9},{9,8},{10,11... | collective-permute-start | bytes 786440 | tf_op jit(solution)/shard_map/ppermute | solution.py:26
  53.4 1.0 collective-permute-start.30
  54.3 0.7 copy-done.9
  55.0 0.7 copy-done.11
  55.7 0.8 collective-permute-start.1
  56.6 0.7 copy-done.13
  57.3 2.8 %collective-permute-start.7 = (bf16[8,128,128]{2,1,0:T(8,128)(2,1)}, bf16[8,128,128]{2,1,0:T(8,128)(2,1)}, u32[]{:S(2)}, u32[]{:S(2)}) collective-permute-start(bf16[8,128,128]{2,1,0:T(8,128)(2,1)} %collective-permute-done.6.rest_0_), channel_id=1, source_target_pairs={{0,2},{1,15},{2,4},{3,1},{4,6},{5,3},{6,8},{7,5},{8,10},{9,7},{10,... | collective-permute-start | bytes 786440 | tf_op jit(solution)/shard_map/ppermute | solution.py:26
  60.1 0.7 copy-done.15
  60.9 2.7 %collective-permute-start.19 = (bf16[8,128,128]{2,1,0:T(8,128)(2,1)}, bf16[8,128,128]{2,1,0:T(8,128)(2,1)S(1)}, u32[]{:S(2)}, u32[]{:S(2)}) collective-permute-start(bf16[8,128,128]{2,1,0:T(8,128)(2,1)} %collective-permute-done.18.rest_1_), channel_id=1, source_target_pairs={{0,2},{1,15},{2,4},{3,1},{4,6},{5,3},{6,8},{7,5},{8,10},{9,7},{10,... | collective-permute-start | bytes 786440 | tf_op jit(solution)/shard_map/ppermute | solution.py:26
  63.5 3.2 %collective-permute-start.24 = (bf16[8,128,128]{2,1,0:T(8,128)(2,1)}, bf16[8,128,128]{2,1,0:T(8,128)(2,1)S(1)}, u32[]{:S(2)}, u32[]{:S(2)}) collective-permute-start(bf16[8,128,128]{2,1,0:T(8,128)(2,1)} %collective-permute-done.13.rest_5_), channel_id=1, source_target_pairs={{0,1},{1,0},{2,3},{3,2},{4,5},{5,4},{6,7},{7,6},{8,9},{9,8},{10,11... | collective-permute-start | bytes 786440 | tf_op jit(solution)/shard_map/ppermute | solution.py:26
  66.9 1.5 %collective-permute-done.22.rest_4_ = bf16[8,128,128]{2,1,0:T(8,128)(2,1)} collective-permute-done((bf16[8,128,128]{2,1,0:T(8,128)(2,1)}, bf16[8,128,128]{2,1,0:T(8,128)(2,1)}, u32[]{:S(2)}, u32[]{:S(2)}) %collective-permute-start.22) | collective-permute-done | bytes 262176 | tf_op jit(solution)/shard_map/ppermute | solution.py:26
  68.4 2.0 %collective-permute-start.8 = (bf16[8,128,128]{2,1,0:T(8,128)(2,1)}, bf16[8,128,128]{2,1,0:T(8,128)(2,1)S(1)}, u32[]{:S(2)}, u32[]{:S(2)}) collective-permute-start(bf16[8,128,128]{2,1,0:T(8,128)(2,1)} %collective-permute-done.7.rest_0_), channel_id=1, source_target_pairs={{0,2},{1,15},{2,4},{3,1},{4,6},{5,3},{6,8},{7,5},{8,10},{9,7},{10,... | collective-permute-start | bytes 786440 | tf_op jit(solution)/shard_map/ppermute | solution.py:26
  70.4 1.0 %copy-done = bf16[4,1,256,256]{3,2,1,0:T(8,128)(2,1)S(1)} copy-done((bf16[4,1,256,256]{3,2,1,0:T(8,128)(2,1)S(1)}, bf16[4,1,256,256]{3,2,1,0:T(8,128)(2,1)}, u32[]{:S(2)}) %copy-start) | copy-done | bytes 524312
  71.4 0.7 copy-done.17
  72.1 0.7 copy-done.18
  72.7 3.2 %mixed.4 = (bf16[4,16,256,512]{3,2,1,0:T(8,128)(2,1)S(1)}, bf16[256,2048]{1,0:T(8,128)(2,1)S(1)}) custom-call(s32[2]{0:T(128)S(1)} %pad_add_fusion.pos, s32[64]{0:T(128)S(1)} %copy-done.17, s32[64]{0:T(128)S(1)} %copy-done.18, bf16[256,8192]{1,0:T(8,128)(2,1)} %psi_ref.1, bf16[4,256,256]{2,1,0:T(8,128)(2,1)S(1)} %bitcast.6), custom_call_target="tpu_custom_call" | custom-call | flops 1073741824 | bytes 6291456 | tf_op jit(solution)/shard_map/mixed/pallas_call | solution.py:87
  76.0 1.3 %mixed.5.kept = bf16[4,16,256,512]{3,2,1,0:T(8,128)(2,1)S(1)} custom-call(bf16[256,2048]{1,0:T(8,128)(2,1)S(1)} %get-tuple-element.7.masked_ref, bf16[4,256,256]{2,1,0:T(8,128)(2,1)S(1)} %collective-permute-done.left, bf16[4,16,256,512]{3,2,1,0:T(8,128)(2,1)S(1)} %get-tuple-element.8.kept), custom_call_target="tpu_custom_call", output_to_operand_aliasing={{}: (2, {})} | custom-call | flops 1073741824 | bytes 6291456 | tf_op jit(solution)/shard_map/mixed/pallas_call | solution.py:107
  77.2 3.0 %collective-permute-start.25 = (bf16[8,128,128]{2,1,0:T(8,128)(2,1)}, bf16[8,128,128]{2,1,0:T(8,128)(2,1)S(1)}, u32[]{:S(2)}, u32[]{:S(2)}) collective-permute-start(bf16[8,128,128]{2,1,0:T(8,128)(2,1)} %collective-permute-done.7.rest_0_), channel_id=1, source_target_pairs={{0,1},{1,0},{2,3},{3,2},{4,5},{5,4},{6,7},{7,6},{8,9},{9,8},{10,11... | collective-permute-start | bytes 786440 | tf_op jit(solution)/shard_map/ppermute | solution.py:26
  80.4 0.4 collective-permute-start.26
  80.8 1.3 %mixed.6.kept = bf16[4,16,256,512]{3,2,1,0:T(8,128)(2,1)S(1)} custom-call(bf16[256,2048]{1,0:T(8,128)(2,1)S(1)} %get-tuple-element.7.masked_ref, bf16[4,256,256]{2,1,0:T(8,128)(2,1)S(1)} %collective-permute-done.2.left, bf16[4,16,256,512]{3,2,1,0:T(8,128)(2,1)S(1)} %mixed.5.kept), custom_call_target="tpu_custom_call", output_to_operand_aliasing={{}: (2, {})} | custom-call | flops 1073741824 | bytes 6291456 | tf_op jit(solution)/shard_map/mixed/pallas_call | solution.py:107
  82.7 1.3 %mixed.7 = bf16[4,16,256,512]{3,2,1,0:T(8,128)(2,1)S(1)} custom-call(bf16[256,2048]{1,0:T(8,128)(2,1)S(1)} %get-tuple-element.7.masked_ref, bf16[4,256,256]{2,1,0:T(8,128)(2,1)S(1)} %collective-permute-done.1.left, bf16[4,16,256,512]{3,2,1,0:T(8,128)(2,1)S(1)} %mixed.6.kept), custom_call_target="tpu_custom_call", output_to_operand_aliasing={{}: (2, {})} | custom-call | flops 1073741824 | bytes 6291456 | tf_op jit(solution)/shard_map/mixed/pallas_call | solution.py:107
  84.1 3.5 %total.4.rest_8_ = f32[256,2048]{1,0:T(8,128)} custom-call(s32[2]{0:T(128)S(1)} %pad_add_fusion.pos, s32[64]{0:T(128)S(1)} %copy-done.17, s32[64]{0:T(128)S(1)} %copy-done.18, bf16[4,16,256,512]{3,2,1,0:T(8,128)(2,1)S(1)} %mixed.7, bf16[8,128,128]{2,1,0:T(8,128)(2,1)S(1)} %constant_dynamic-update-slice_fusion.rest_0_, ...), custom_call_target="tpu_custom_call" | custom-call | flops 805306368 | bytes 4194304 | tf_op jit(solution)/shard_map/total/pallas_call | solution.py:174
  87.6 4.1 %total.5.rest_8_ = f32[256,2048]{1,0:T(8,128)} custom-call(s32[2]{0:T(128)S(1)} %pad_add_fusion.pos, s32[64]{0:T(128)S(1)} %copy-done.17, s32[64]{0:T(128)S(1)} %copy-done.18, bf16[4,16,256,512]{3,2,1,0:T(8,128)(2,1)S(1)} %mixed.7, bf16[8,128,128]{2,1,0:T(8,128)(2,1)} %collective-permute-done.6.rest_0_, ...), custom_call_target="tpu_custom_call", output_to_operand_aliasing={{}: (12, {})} | custom-call | flops 536870912 | bytes 4194304 | tf_op jit(solution)/shard_map/total/pallas_call | solution.py:174
  91.7 3.9 %total.6.rest_4_ = f32[256,2048]{1,0:T(8,128)} custom-call(s32[2]{0:T(128)S(1)} %pad_add_fusion.pos, s32[64]{0:T(128)S(1)} %copy-done.17, s32[64]{0:T(128)S(1)} %copy-done.18, bf16[4,16,256,512]{3,2,1,0:T(8,128)(2,1)S(1)} %mixed.7, bf16[8,128,128]{2,1,0:T(8,128)(2,1)} %collective-permute-done.7.rest_0_, ...), custom_call_target="tpu_custom_call", output_to_operand_aliasing={{}: (12, {})} | custom-call | flops 536870912 | bytes 4194304 | tf_op jit(solution)/shard_map/total/pallas_call | solution.py:174
  95.6 2.0 %total.7 = f32[256,2048]{1,0:T(8,128)} custom-call(s32[2]{0:T(128)S(1)} %pad_add_fusion.pos, s32[64]{0:T(128)S(1)} %copy-done.17, s32[64]{0:T(128)S(1)} %copy-done.18, bf16[4,16,256,512]{3,2,1,0:T(8,128)(2,1)S(1)} %mixed.7, bf16[8,128,128]{2,1,0:T(8,128)(2,1)S(1)} %collective-permute-done.8.rest_0_, ...), custom_call_target="tpu_custom_call", output_to_operand_aliasing={{}: (8, {})} | custom-call | flops 268435456 | bytes 4194304 | tf_op jit(solution)/shard_map/total/pallas_call | solution.py:174
  (77 shorter events, 1.1 us)
Async XLA Ops:
  0.0 13.2 %collective-permute-start.3 = (bf16[4,128,128]{2,1,0:T(8,128)(2,1)}, bf16[4,128,128]{2,1,0:T(8,128)(2,1)S(1)}, u32[]{:S(2)}, u32[]{:S(2)}) collective-permute-start(bf16[4,128,128]{2,1,0:T(8,128)(2,1)} %bitcast.7), channel_id=1, source_target_pairs={{0,0},{1,1},{2,2},{3,3},{4,4},{5,5},{6,6},{7,7},{8,8},{9,9},{10,10... | collective-permute-start | bytes 393224 | tf_op jit(solution)/shard_map/ppermute | solution.py:26
  1.6 11.7 %collective-permute-start.4 = (bf16[4,128,128]{2,1,0:T(8,128)(2,1)}, bf16[4,128,128]{2,1,0:T(8,128)(2,1)S(1)}, u32[]{:S(2)}, u32[]{:S(2)}) collective-permute-start(bf16[4,128,128]{2,1,0:T(8,128)(2,1)} %bitcast.8), channel_id=1, source_target_pairs={{0,16},{1,17},{2,18},{3,19},{4,20},{5,21},{6,22},{7,23},{8,24},{9,... | collective-permute-start | bytes 393224 | tf_op jit(solution)/shard_map/ppermute | solution.py:26
  6.2 8.7 %collective-permute-start.9 = (bf16[4,128,128]{2,1,0:T(8,128)(2,1)}, bf16[4,128,128]{2,1,0:T(8,128)(2,1)S(1)}, u32[]{:S(2)}, u32[]{:S(2)}) collective-permute-start(bf16[4,128,128]{2,1,0:T(8,128)(2,1)} %bitcast.9), channel_id=1, source_target_pairs={{0,32},{1,33},{2,34},{3,35},{4,36},{5,37},{6,38},{7,39},{8,40},{9,... | collective-permute-start | bytes 393224 | tf_op jit(solution)/shard_map/ppermute | solution.py:26
  8.6 9.3 %collective-permute-start.10 = (bf16[4,128,128]{2,1,0:T(8,128)(2,1)}, bf16[4,128,128]{2,1,0:T(8,128)(2,1)S(1)}, u32[]{:S(2)}, u32[]{:S(2)}) collective-permute-start(bf16[4,128,128]{2,1,0:T(8,128)(2,1)} %bitcast.10), channel_id=1, source_target_pairs={{0,48},{1,49},{2,50},{3,51},{4,52},{5,53},{6,54},{7,55},{8,56},{9,... | collective-permute-start | bytes 393224 | tf_op jit(solution)/shard_map/ppermute | solution.py:26
  13.2 13.3 %collective-permute-start.20 = (bf16[8,128,128]{2,1,0:T(8,128)(2,1)S(1)}, bf16[8,128,128]{2,1,0:T(8,128)(2,1)S(1)}, u32[]{:S(2)}, u32[]{:S(2)}) collective-permute-start(bf16[8,128,128]{2,1,0:T(8,128)(2,1)S(1)} %constant_dynamic-update-slice_fusion.rest_0_), channel_id=1, source_target_pairs={{0,14},{1,3},{2,0},{3,5},{4,2},{5,7},{6,4},{7,9},{8,6},{9,11},{10,... | collective-permute-start | bytes 786440 | tf_op jit(solution)/shard_map/ppermute | solution.py:26
  17.9 10.0 %collective-permute-start.11 = (bf16[8,128,128]{2,1,0:T(8,128)(2,1)S(1)}, bf16[8,128,128]{2,1,0:T(8,128)(2,1)S(1)}, u32[]{:S(2)}, u32[]{:S(2)}) collective-permute-start(bf16[8,128,128]{2,1,0:T(8,128)(2,1)S(1)} %constant_dynamic-update-slice_fusion.2.rest_1_), channel_id=1, source_target_pairs={{0,14},{1,3},{2,0},{3,5},{4,2},{5,7},{6,4},{7,9},{8,6},{9,11},{10,... | collective-permute-start | bytes 786440 | tf_op jit(solution)/shard_map/ppermute | solution.py:26
  19.6 11.7 %collective-permute-start.5 = (bf16[8,128,128]{2,1,0:T(8,128)(2,1)S(1)}, bf16[8,128,128]{2,1,0:T(8,128)(2,1)S(1)}, u32[]{:S(2)}, u32[]{:S(2)}) collective-permute-start(bf16[8,128,128]{2,1,0:T(8,128)(2,1)S(1)} %constant_dynamic-update-slice_fusion.rest_0_), channel_id=1, source_target_pairs={{0,2},{1,15},{2,4},{3,1},{4,6},{5,3},{6,8},{7,5},{8,10},{9,7},{10,... | collective-permute-start | bytes 786440 | tf_op jit(solution)/shard_map/ppermute | solution.py:26
  23.6 14.4 %collective-permute-start = (bf16[4,256,256]{2,1,0:T(8,128)(2,1)}, bf16[4,256,256]{2,1,0:T(8,128)(2,1)S(1)}, u32[]{:S(2)}, u32[]{:S(2)}) collective-permute-start(bf16[4,256,256]{2,1,0:T(8,128)(2,1)} %bitcast.4), channel_id=1, source_target_pairs={{0,192},{1,65},{2,194},{3,67},{4,196},{5,69},{6,198},{7,71},{8,200... | collective-permute-start | bytes 1572872 | tf_op jit(solution)/shard_map/ppermute | solution.py:26
  23.7 14.5 %collective-permute-start.2 = (bf16[4,256,256]{2,1,0:T(8,128)(2,1)}, bf16[4,256,256]{2,1,0:T(8,128)(2,1)S(1)}, u32[]{:S(2)}, u32[]{:S(2)}) collective-permute-start(bf16[4,256,256]{2,1,0:T(8,128)(2,1)} %bitcast.5), channel_id=1, source_target_pairs={{0,64},{1,193},{2,66},{3,195},{4,68},{5,197},{6,70},{7,199},{8,72}... | collective-permute-start | bytes 1572872 | tf_op jit(solution)/shard_map/ppermute | solution.py:26
  26.6 6.3 %collective-permute-start.17 = (bf16[8,128,128]{2,1,0:T(8,128)(2,1)S(1)}, bf16[8,128,128]{2,1,0:T(8,128)(2,1)S(1)}, u32[]{:S(2)}, u32[]{:S(2)}) collective-permute-start(bf16[8,128,128]{2,1,0:T(8,128)(2,1)S(1)} %constant_dynamic-update-slice_fusion.2.rest_1_), channel_id=1, source_target_pairs={{0,2},{1,15},{2,4},{3,1},{4,6},{5,3},{6,8},{7,5},{8,10},{9,7},{10,... | collective-permute-start | bytes 786440 | tf_op jit(solution)/shard_map/ppermute | solution.py:26
  27.9 8.9 %collective-permute-start.31 = (bf16[8,128,128]{2,1,0:T(8,128)(2,1)S(1)}, bf16[8,128,128]{2,1,0:T(8,128)(2,1)S(1)}, u32[]{:S(2)}, u32[]{:S(2)}) collective-permute-start(bf16[8,128,128]{2,1,0:T(8,128)(2,1)S(1)} %constant_dynamic-update-slice_fusion.rest_0_), channel_id=1, source_target_pairs={{0,1},{1,0},{2,3},{3,2},{4,5},{5,4},{6,7},{7,6},{8,9},{9,8},{10,11... | collective-permute-start | bytes 786440 | tf_op jit(solution)/shard_map/ppermute | solution.py:26
  31.3 5.5 %collective-permute-start.32 = (bf16[8,128,128]{2,1,0:T(8,128)(2,1)S(1)}, bf16[8,128,128]{2,1,0:T(8,128)(2,1)S(1)}, u32[]{:S(2)}, u32[]{:S(2)}) collective-permute-start(bf16[8,128,128]{2,1,0:T(8,128)(2,1)S(1)} %constant_dynamic-update-slice_fusion.2.rest_1_), channel_id=1, source_target_pairs={{0,1},{1,0},{2,3},{3,2},{4,5},{5,4},{6,7},{7,6},{8,9},{9,8},{10,11... | collective-permute-start | bytes 786440 | tf_op jit(solution)/shard_map/ppermute | solution.py:26
  32.9 5.3 %collective-permute-start.33 = (bf16[8,128,128]{2,1,0:T(8,128)(2,1)S(1)}, bf16[8,128,128]{2,1,0:T(8,128)(2,1)S(1)}, u32[]{:S(2)}, u32[]{:S(2)}) collective-permute-start(bf16[8,128,128]{2,1,0:T(8,128)(2,1)S(1)} %collective-permute-done.20.rest_8_), channel_id=1, source_target_pairs={{0,1},{1,0},{2,3},{3,2},{4,5},{5,4},{6,7},{7,6},{8,9},{9,8},{10,11... | collective-permute-start | bytes 786440 | tf_op jit(solution)/shard_map/ppermute | solution.py:26
  36.9 4.7 %collective-permute-start.34 = (bf16[8,128,128]{2,1,0:T(8,128)(2,1)S(1)}, bf16[8,128,128]{2,1,0:T(8,128)(2,1)S(1)}, u32[]{:S(2)}, u32[]{:S(2)}) collective-permute-start(bf16[8,128,128]{2,1,0:T(8,128)(2,1)S(1)} %collective-permute-done.11.rest_9_), channel_id=1, source_target_pairs={{0,1},{1,0},{2,3},{3,2},{4,5},{5,4},{6,7},{7,6},{8,9},{9,8},{10,11... | collective-permute-start | bytes 786440 | tf_op jit(solution)/shard_map/ppermute | solution.py:26
  37.6 6.1 %collective-permute-start.35 = (bf16[8,128,128]{2,1,0:T(8,128)(2,1)S(1)}, bf16[8,128,128]{2,1,0:T(8,128)(2,1)S(1)}, u32[]{:S(2)}, u32[]{:S(2)}) collective-permute-start(bf16[8,128,128]{2,1,0:T(8,128)(2,1)S(1)} %collective-permute-done.5.rest_4_), channel_id=1, source_target_pairs={{0,1},{1,0},{2,3},{3,2},{4,5},{5,4},{6,7},{7,6},{8,9},{9,8},{10,11... | collective-permute-start | bytes 786440 | tf_op jit(solution)/shard_map/ppermute | solution.py:26
  38.1 7.2 %collective-permute-start.21 = (bf16[8,128,128]{2,1,0:T(8,128)(2,1)S(1)}, bf16[8,128,128]{2,1,0:T(8,128)(2,1)}, u32[]{:S(2)}, u32[]{:S(2)}) collective-permute-start(bf16[8,128,128]{2,1,0:T(8,128)(2,1)S(1)} %collective-permute-done.20.rest_8_), channel_id=1, source_target_pairs={{0,14},{1,3},{2,0},{3,5},{4,2},{5,7},{6,4},{7,9},{8,6},{9,11},{10,... | collective-permute-start | bytes 786440 | tf_op jit(solution)/shard_map/ppermute | solution.py:26
  38.1 10.2 %collective-permute-start.12 = (bf16[8,128,128]{2,1,0:T(8,128)(2,1)S(1)}, bf16[8,128,128]{2,1,0:T(8,128)(2,1)}, u32[]{:S(2)}, u32[]{:S(2)}) collective-permute-start(bf16[8,128,128]{2,1,0:T(8,128)(2,1)S(1)} %collective-permute-done.11.rest_9_), channel_id=1, source_target_pairs={{0,14},{1,3},{2,0},{3,5},{4,2},{5,7},{6,4},{7,9},{8,6},{9,11},{10,... | collective-permute-start | bytes 786440 | tf_op jit(solution)/shard_map/ppermute | solution.py:26
  38.2 0.7 copy-start.3
  38.9 14.4 %collective-permute-start.6 = (bf16[8,128,128]{2,1,0:T(8,128)(2,1)S(1)}, bf16[8,128,128]{2,1,0:T(8,128)(2,1)}, u32[]{:S(2)}, u32[]{:S(2)}) collective-permute-start(bf16[8,128,128]{2,1,0:T(8,128)(2,1)S(1)} %collective-permute-done.5.rest_4_), channel_id=1, source_target_pairs={{0,2},{1,15},{2,4},{3,1},{4,6},{5,3},{6,8},{7,5},{8,10},{9,7},{10,... | collective-permute-start | bytes 786440 | tf_op jit(solution)/shard_map/ppermute | solution.py:26
  42.3 11.1 %collective-permute-start.18 = (bf16[8,128,128]{2,1,0:T(8,128)(2,1)S(1)}, bf16[8,128,128]{2,1,0:T(8,128)(2,1)}, u32[]{:S(2)}, u32[]{:S(2)}) collective-permute-start(bf16[8,128,128]{2,1,0:T(8,128)(2,1)S(1)} %collective-permute-done.17.rest_5_), channel_id=1, source_target_pairs={{0,2},{1,15},{2,4},{3,1},{4,6},{5,3},{6,8},{7,5},{8,10},{9,7},{10,... | collective-permute-start | bytes 786440 | tf_op jit(solution)/shard_map/ppermute | solution.py:26
  44.4 9.9 %collective-permute-start.36 = (bf16[8,128,128]{2,1,0:T(8,128)(2,1)S(1)}, bf16[8,128,128]{2,1,0:T(8,128)(2,1)S(1)}, u32[]{:S(2)}, u32[]{:S(2)}) collective-permute-start(bf16[8,128,128]{2,1,0:T(8,128)(2,1)S(1)} %collective-permute-done.17.rest_5_), channel_id=1, source_target_pairs={{0,1},{1,0},{2,3},{3,2},{4,5},{5,4},{6,7},{7,6},{8,9},{9,8},{10,11... | collective-permute-start | bytes 786440 | tf_op jit(solution)/shard_map/ppermute | solution.py:26
  45.3 9.8 %collective-permute-start.27 = (bf16[8,128,128]{2,1,0:T(8,128)(2,1)}, bf16[8,128,128]{2,1,0:T(8,128)(2,1)S(1)}, u32[]{:S(2)}, u32[]{:S(2)}) collective-permute-start(bf16[8,128,128]{2,1,0:T(8,128)(2,1)} %collective-permute-done.21.rest_4_), channel_id=1, source_target_pairs={{0,1},{1,0},{2,3},{3,2},{4,5},{5,4},{6,7},{7,6},{8,9},{9,8},{10,11... | collective-permute-start | bytes 786440 | tf_op jit(solution)/shard_map/ppermute | solution.py:26
  48.3 8.3 %collective-permute-start.28 = (bf16[8,128,128]{2,1,0:T(8,128)(2,1)}, bf16[8,128,128]{2,1,0:T(8,128)(2,1)S(1)}, u32[]{:S(2)}, u32[]{:S(2)}) collective-permute-start(bf16[8,128,128]{2,1,0:T(8,128)(2,1)} %collective-permute-done.12.rest_5_), channel_id=1, source_target_pairs={{0,1},{1,0},{2,3},{3,2},{4,5},{5,4},{6,7},{7,6},{8,9},{9,8},{10,11... | collective-permute-start | bytes 786440 | tf_op jit(solution)/shard_map/ppermute | solution.py:26
  53.4 6.7 %collective-permute-start.29 = (bf16[8,128,128]{2,1,0:T(8,128)(2,1)}, bf16[8,128,128]{2,1,0:T(8,128)(2,1)S(1)}, u32[]{:S(2)}, u32[]{:S(2)}) collective-permute-start(bf16[8,128,128]{2,1,0:T(8,128)(2,1)} %collective-permute-done.6.rest_0_), channel_id=1, source_target_pairs={{0,1},{1,0},{2,3},{3,2},{4,5},{5,4},{6,7},{7,6},{8,9},{9,8},{10,11... | collective-permute-start | bytes 786440 | tf_op jit(solution)/shard_map/ppermute | solution.py:26
  53.4 7.5 %collective-permute-start.30 = (bf16[8,128,128]{2,1,0:T(8,128)(2,1)}, bf16[8,128,128]{2,1,0:T(8,128)(2,1)}, u32[]{:S(2)}, u32[]{:S(2)}) collective-permute-start(bf16[8,128,128]{2,1,0:T(8,128)(2,1)} %collective-permute-done.18.rest_1_), channel_id=1, source_target_pairs={{0,1},{1,0},{2,3},{3,2},{4,5},{5,4},{6,7},{7,6},{8,9},{9,8},{10,11... | collective-permute-start | bytes 786440 | tf_op jit(solution)/shard_map/ppermute | solution.py:26
  55.0 8.5 %collective-permute-start.13 = (bf16[8,128,128]{2,1,0:T(8,128)(2,1)}, bf16[8,128,128]{2,1,0:T(8,128)(2,1)}, u32[]{:S(2)}, u32[]{:S(2)}) collective-permute-start(bf16[8,128,128]{2,1,0:T(8,128)(2,1)} %collective-permute-done.12.rest_5_), channel_id=1, source_target_pairs={{0,14},{1,3},{2,0},{3,5},{4,2},{5,7},{6,4},{7,9},{8,6},{9,11},{10,... | collective-permute-start | bytes 786440 | tf_op jit(solution)/shard_map/ppermute | solution.py:26
  55.7 24.6 %collective-permute-start.1 = (bf16[4,256,256]{2,1,0:T(8,128)(2,1)S(1)}, bf16[4,256,256]{2,1,0:T(8,128)(2,1)S(1)}, u32[]{:S(2)}, u32[]{:S(2)}) collective-permute-start(bf16[4,256,256]{2,1,0:T(8,128)(2,1)S(1)} %collective-permute-done.left), channel_id=1, source_target_pairs={{0,192},{1,65},{2,194},{3,67},{4,196},{5,69},{6,198},{7,71},{8,200... | collective-permute-start | bytes 1572872 | tf_op jit(solution)/shard_map/ppermute | solution.py:26
  57.3 9.6 %collective-permute-start.7 = (bf16[8,128,128]{2,1,0:T(8,128)(2,1)}, bf16[8,128,128]{2,1,0:T(8,128)(2,1)}, u32[]{:S(2)}, u32[]{:S(2)}) collective-permute-start(bf16[8,128,128]{2,1,0:T(8,128)(2,1)} %collective-permute-done.6.rest_0_), channel_id=1, source_target_pairs={{0,2},{1,15},{2,4},{3,1},{4,6},{5,3},{6,8},{7,5},{8,10},{9,7},{10,... | collective-permute-start | bytes 786440 | tf_op jit(solution)/shard_map/ppermute | solution.py:26
  60.1 0.7 copy-start.15
  60.8 7.5 %collective-permute-start.22 = (bf16[8,128,128]{2,1,0:T(8,128)(2,1)}, bf16[8,128,128]{2,1,0:T(8,128)(2,1)}, u32[]{:S(2)}, u32[]{:S(2)}) collective-permute-start(bf16[8,128,128]{2,1,0:T(8,128)(2,1)} %collective-permute-done.21.rest_4_), channel_id=1, source_target_pairs={{0,14},{1,3},{2,0},{3,5},{4,2},{5,7},{6,4},{7,9},{8,6},{9,11},{10,... | collective-permute-start | bytes 786440 | tf_op jit(solution)/shard_map/ppermute | solution.py:26
  60.9 16.4 %collective-permute-start.19 = (bf16[8,128,128]{2,1,0:T(8,128)(2,1)}, bf16[8,128,128]{2,1,0:T(8,128)(2,1)S(1)}, u32[]{:S(2)}, u32[]{:S(2)}) collective-permute-start(bf16[8,128,128]{2,1,0:T(8,128)(2,1)} %collective-permute-done.18.rest_1_), channel_id=1, source_target_pairs={{0,2},{1,15},{2,4},{3,1},{4,6},{5,3},{6,8},{7,5},{8,10},{9,7},{10,... | collective-permute-start | bytes 786440 | tf_op jit(solution)/shard_map/ppermute | solution.py:26
  63.5 16.9 %collective-permute-start.24 = (bf16[8,128,128]{2,1,0:T(8,128)(2,1)}, bf16[8,128,128]{2,1,0:T(8,128)(2,1)S(1)}, u32[]{:S(2)}, u32[]{:S(2)}) collective-permute-start(bf16[8,128,128]{2,1,0:T(8,128)(2,1)} %collective-permute-done.13.rest_5_), channel_id=1, source_target_pairs={{0,1},{1,0},{2,3},{3,2},{4,5},{5,4},{6,7},{7,6},{8,9},{9,8},{10,11... | collective-permute-start | bytes 786440 | tf_op jit(solution)/shard_map/ppermute | solution.py:26
  66.8 15.5 %collective-permute-start.14 = (bf16[8,128,128]{2,1,0:T(8,128)(2,1)}, bf16[8,128,128]{2,1,0:T(8,128)(2,1)S(1)}, u32[]{:S(2)}, u32[]{:S(2)}) collective-permute-start(bf16[8,128,128]{2,1,0:T(8,128)(2,1)} %collective-permute-done.13.rest_5_), channel_id=1, source_target_pairs={{0,14},{1,3},{2,0},{3,5},{4,2},{5,7},{6,4},{7,9},{8,6},{9,11},{10,... | collective-permute-start | bytes 786440 | tf_op jit(solution)/shard_map/ppermute | solution.py:26
  68.4 13.7 %collective-permute-start.8 = (bf16[8,128,128]{2,1,0:T(8,128)(2,1)}, bf16[8,128,128]{2,1,0:T(8,128)(2,1)S(1)}, u32[]{:S(2)}, u32[]{:S(2)}) collective-permute-start(bf16[8,128,128]{2,1,0:T(8,128)(2,1)} %collective-permute-done.7.rest_0_), channel_id=1, source_target_pairs={{0,2},{1,15},{2,4},{3,1},{4,6},{5,3},{6,8},{7,5},{8,10},{9,7},{10,... | collective-permute-start | bytes 786440 | tf_op jit(solution)/shard_map/ppermute | solution.py:26
  70.4 1.0 %copy-start = (bf16[4,1,256,256]{3,2,1,0:T(8,128)(2,1)S(1)}, bf16[4,1,256,256]{3,2,1,0:T(8,128)(2,1)}, u32[]{:S(2)}) copy-start(bf16[4,1,256,256]{3,2,1,0:T(8,128)(2,1)} %param.6) | copy-start | bytes 1572868
  77.2 14.4 %collective-permute-start.25 = (bf16[8,128,128]{2,1,0:T(8,128)(2,1)}, bf16[8,128,128]{2,1,0:T(8,128)(2,1)S(1)}, u32[]{:S(2)}, u32[]{:S(2)}) collective-permute-start(bf16[8,128,128]{2,1,0:T(8,128)(2,1)} %collective-permute-done.7.rest_0_), channel_id=1, source_target_pairs={{0,1},{1,0},{2,3},{3,2},{4,5},{5,4},{6,7},{7,6},{8,9},{9,8},{10,11... | collective-permute-start | bytes 786440 | tf_op jit(solution)/shard_map/ppermute | solution.py:26
  80.3 11.4 %collective-permute-start.23 = (bf16[8,128,128]{2,1,0:T(8,128)(2,1)}, bf16[8,128,128]{2,1,0:T(8,128)(2,1)S(1)}, u32[]{:S(2)}, u32[]{:S(2)}) collective-permute-start(bf16[8,128,128]{2,1,0:T(8,128)(2,1)} %collective-permute-done.22.rest_4_), channel_id=1, source_target_pairs={{0,1},{1,0},{2,3},{3,2},{4,5},{5,4},{6,7},{7,6},{8,9},{9,8},{10,11... | collective-permute-start | bytes 786440 | tf_op jit(solution)/shard_map/ppermute | solution.py:26
  80.4 11.3 %collective-permute-start.26 = (bf16[8,128,128]{2,1,0:T(8,128)(2,1)S(1)}, bf16[8,128,128]{2,1,0:T(8,128)(2,1)S(1)}, u32[]{:S(2)}, u32[]{:S(2)}) collective-permute-start(bf16[8,128,128]{2,1,0:T(8,128)(2,1)S(1)} %collective-permute-done.19.rest_1_), channel_id=1, source_target_pairs={{0,1},{1,0},{2,3},{3,2},{4,5},{5,4},{6,7},{7,6},{8,9},{9,8},{10,11... | collective-permute-start | bytes 786440 | tf_op jit(solution)/shard_map/ppermute | solution.py:26
  82.1 1.9 %copy-start.2 = (bf16[8,128,128]{2,1,0:T(8,128)(2,1)S(1)}, bf16[8,128,128]{2,1,0:T(8,128)(2,1)}, u32[]{:S(2)}) copy-start(bf16[8,128,128]{2,1,0:T(8,128)(2,1)} %copy-done.1) | copy-start | bytes 786436
  82.1 1.9 %copy-start.4 = (bf16[8,128,128]{2,1,0:T(8,128)(2,1)S(1)}, bf16[8,128,128]{2,1,0:T(8,128)(2,1)}, u32[]{:S(2)}) copy-start(bf16[8,128,128]{2,1,0:T(8,128)(2,1)} %copy-done.3) | copy-start | bytes 786436
  82.1 1.9 %copy-start.6 = (bf16[8,128,128]{2,1,0:T(8,128)(2,1)S(1)}, bf16[8,128,128]{2,1,0:T(8,128)(2,1)}, u32[]{:S(2)}) copy-start(bf16[8,128,128]{2,1,0:T(8,128)(2,1)} %copy-done.5) | copy-start | bytes 786436
  82.1 1.9 %copy-start.8 = (bf16[8,128,128]{2,1,0:T(8,128)(2,1)S(1)}, bf16[8,128,128]{2,1,0:T(8,128)(2,1)}, u32[]{:S(2)}) copy-start(bf16[8,128,128]{2,1,0:T(8,128)(2,1)} %copy-done.7) | copy-start | bytes 786436
  82.1 1.9 %copy-start.10 = (bf16[8,128,128]{2,1,0:T(8,128)(2,1)S(1)}, bf16[8,128,128]{2,1,0:T(8,128)(2,1)}, u32[]{:S(2)}) copy-start(bf16[8,128,128]{2,1,0:T(8,128)(2,1)} %copy-done.9) | copy-start | bytes 786436
  82.1 13.5 %collective-permute-start.15 = (bf16[8,128,128]{2,1,0:T(8,128)(2,1)S(1)}, bf16[8,128,128]{2,1,0:T(8,128)(2,1)S(1)}, u32[]{:S(2)}, u32[]{:S(2)}) collective-permute-start(bf16[8,128,128]{2,1,0:T(8,128)(2,1)S(1)} %collective-permute-done.8.rest_0_), channel_id=1, source_target_pairs={{0,1},{1,0},{2,3},{3,2},{4,5},{5,4},{6,7},{7,6},{8,9},{9,8},{10,11... | collective-permute-start | bytes 786440 | tf_op jit(solution)/shard_map/ppermute | solution.py:26
  82.3 13.3 %collective-permute-start.16 = (bf16[8,128,128]{2,1,0:T(8,128)(2,1)S(1)}, bf16[8,128,128]{2,1,0:T(8,128)(2,1)S(1)}, u32[]{:S(2)}, u32[]{:S(2)}) collective-permute-start(bf16[8,128,128]{2,1,0:T(8,128)(2,1)S(1)} %collective-permute-done.14.rest_1_), channel_id=1, source_target_pairs={{0,1},{1,0},{2,3},{3,2},{4,5},{5,4},{6,7},{7,6},{8,9},{9,8},{10,11... | collective-permute-start | bytes 786440 | tf_op jit(solution)/shard_map/ppermute | solution.py:26
  84.0 3.6 %copy-start.12 = (bf16[8,128,128]{2,1,0:T(8,128)(2,1)S(1)}, bf16[8,128,128]{2,1,0:T(8,128)(2,1)}, u32[]{:S(2)}) copy-start(bf16[8,128,128]{2,1,0:T(8,128)(2,1)} %copy-done.11) | copy-start | bytes 786436
  84.1 3.6 %copy-start.14 = (bf16[8,128,128]{2,1,0:T(8,128)(2,1)S(1)}, bf16[8,128,128]{2,1,0:T(8,128)(2,1)}, u32[]{:S(2)}) copy-start(bf16[8,128,128]{2,1,0:T(8,128)(2,1)} %copy-done.13) | copy-start | bytes 786436
  84.1 3.6 %copy-start.16 = (bf16[8,128,128]{2,1,0:T(8,128)(2,1)S(1)}, bf16[8,128,128]{2,1,0:T(8,128)(2,1)}, u32[]{:S(2)}) copy-start(bf16[8,128,128]{2,1,0:T(8,128)(2,1)} %copy-done.15) | copy-start | bytes 786436
  (8 other events, 5.5 us)
where the time goes:
time: 97.8 us; the launch traced here: 97.6 us
  starting transfers between devices  63.5 us (65%)
  Pallas kernels  20.4 us (21%)
  local copies, waits for them, and re-layouts  8.07 us (8%)
  waiting for transfers between devices  5.2 us (5%)
    ppermute x37, starting transfers between devices, permute(): return lax.ppermute(value, AXES, pairs)  63.5 us
    pallas_call x4, Pallas kernels, total_step(): pl.pallas_call(functools.partial(total_kernel, steps), grid_spec=pltpu.Pr...  13.4 us
    unnamed x40, local copies, waits for them, and re-layouts  8.03 us
    ppermute x37, waiting for transfers between devices, permute(): return lax.ppermute(value, AXES, pairs)  5.2 us
    pallas_call x3, Pallas kernels, next_step(): pl.pallas_call(functools.partial(next_kernel, d, size), in_specs=[vmem, v...  3.77 us
    pallas_call x1, Pallas kernels, first_step(): pl.pallas_call(functools.partial(first_kernel, size), grid_spec=pltpu.Pre...  3.21 us
  transfers between devices with their start and end apart: 37, of which 3 were waited for; matrix products, arithmetic and copies ran while one was open for 0% of the time, Pallas kernels for 19%

commit v1 on v0

--- a/solution.py
+++ b/solution.py
@@ -36,6 +36,14 @@
 
 def along_z(d):
     return lambda x, y, z, c: (x, y, z + d * (1 - 2 * c), c)
+
+
+def along_x(x, y, z, c):
+    return (x - 1 + 2 * c, y, z, c)
+
+
+def along_xz(x, y, z, c):
+    return (x - 1 + 2 * c, y, z + 1 - 2 * c, c)
 
 
 def swap_core(x, y, z, c):
@@ -138,11 +146,11 @@
     def one(oa, ob, pa, pb):
         for which, parts in ((core, (oa, ob)), (1 - core, (pa, pb))):
             total = None
-            for k in range(X):
-                ref = parts[k // 2]
+            for n in range(X):
+                ref, h = parts[n // 2], n % 2
+                k = 2 * h + 1 if n < 2 else 2 * h + 2 * which
                 terms = ref.shape[0] // 2
-                at = (k % 2) * terms
-                rcat = jnp.concatenate([ref[at + t] for t in range(terms)], axis=1)
+                rcat = jnp.concatenate([ref[h * terms + t] for t in range(terms)], axis=1)
                 part = lax.dot_general(
                     mixed[((y - x + k) * (1 - 2 * core)) & (Y - 1), z * C + which],
                     rcat,
@@ -198,24 +206,23 @@
     mine = right_env.reshape(terms, size, size)
     left = left_env.reshape(terms, rank, rank)
 
-    groups = [permute(mine, spread(k)) for k in range(X)]
+    groups = [permute(mine, spread(k)) for k in (1, 3)]
     lefts = {0: left, 1: permute(left, along_y(1)), 3: permute(left, along_y(-1))}
     lefts[2] = permute(lefts[1], along_y(1))
 
-    a = {0: jnp.concatenate(groups[:2], axis=0)}
-    b = {0: jnp.concatenate(groups[2:], axis=0)}
-    for r in (1, 2, 3):
-        for chain in (a, b):
-            chain[r] = permute(chain[r - 1], along_z(1))
-            chain[-r] = permute(chain[1 - r], along_z(-1))
-    a[4] = permute(a[3], along_z(1))
-    b[4] = permute(b[-3], along_z(-1))
+    a = {0: jnp.concatenate(groups, axis=0)}
+    for r in (1, 2, 3, 4):
+        a[r] = permute(a[r - 1], along_z(1))
+        if r < 4:
+            a[-r] = permute(a[1 - r], along_z(-1))
+    b = {e: permute(a[e], along_x) for e in a if e < 4}
+    b[4] = permute(a[3], along_xz)
 
     mixed, masked = first_step(scalars, psi, left, size)
     for d in (1, 3, 2):
         mixed = next_step(d, masked, lefts[d], size, mixed)
     out = None
-    for steps in ((0, 1, -1), (2, -2), (3, -3), (4,)):
+    for steps in ((0, 1, -1), (2, -2), (3, -3, 4)):
         rights = []
         for e in steps:
             twin = e if e in (0, 4) else -e

time: 97.8 us -> 89.4 us (0.914)
  starting transfers between devices: 63.5 us -> 52.8 us
  waiting for transfers between devices: 5.2 us -> 9.5 us
  Pallas kernels: 20.4 us -> 19.3 us
    ppermute x37 -> x36, starting transfers between devices: 63.5 us -> 52.8 us  [permute(): return lax.ppermute(value, AXES, pairs)]
    ppermute x37 -> x36, waiting for transfers between devices: 5.2 us -> 9.5 us  [permute(): return lax.ppermute(value, AXES, pairs)]
    pallas_call x4 -> x3, Pallas kernels: 13.4 us -> 12.3 us  [total_step(): pl.pallas_call(functools.partial(total_kernel, steps), grid_spec=pltpu.Pr...]
    unnamed x40 -> x35, local copies, waits for them, and re-layouts: 8.03 us -> 7.27 us
  transfers between devices with their start and end apart: 37 -> 36, of which waited for: 3 -> 4; matrix products, arithmetic and copies ran while one was open for 0% -> 0% of each run, Pallas kernels for 19% -> 16%
where the time goes in v1:
time: 89.4 us; the launch traced here: 89.2 us
  starting transfers between devices  52.8 us (59%)
  Pallas kernels  19.3 us (22%)
  waiting for transfers between devices  9.5 us (11%)
  local copies, waits for them, and re-layouts  7.29 us (8%)
    ppermute x36, starting transfers between devices, permute(): return lax.ppermute(value, AXES, pairs)  52.8 us
    pallas_call x3, Pallas kernels, total_step(): pl.pallas_call(functools.partial(total_kernel, steps), grid_spec=pltpu.Pr...  12.3 us
    ppermute x36, waiting for transfers between devices, permute(): return lax.ppermute(value, AXES, pairs)  9.5 us
    unnamed x35, local copies, waits for them, and re-layouts  7.27 us
    pallas_call x3, Pallas kernels, next_step(): pl.pallas_call(functools.partial(next_kernel, d, size), in_specs=[vmem, v...  3.77 us
    pallas_call x1, Pallas kernels, first_step(): pl.pallas_call(functools.partial(first_kernel, size), grid_spec=pltpu.Pre...  3.21 us
  transfers between devices with their start and end apart: 36, of which 4 were waited for; matrix products, arithmetic and copies ran while one was open for 0% of the time, Pallas kernels for 16%

profile of v1, /device:TPU:1, one launch (start us, length us, event | category | flops | bytes accessed | tf_op | source)
XLA Modules:
  0.0 89.2 jit_solution(11281213591332111395)
XLA Ops:
  0.0 2.0 %collective-permute-start.3 = (bf16[4,128,128]{2,1,0:T(8,128)(2,1)}, bf16[4,128,128]{2,1,0:T(8,128)(2,1)S(1)}, u32[]{:S(2)}, u32[]{:S(2)}) collective-permute-start(bf16[4,128,128]{2,1,0:T(8,128)(2,1)} %bitcast.7), channel_id=1, source_target_pairs={{0,16},{1,17},{2,18},{3,19},{4,20},{5,21},{6,22},{7,23},{8,24},{9,... | collective-permute-start | bytes 393224 | tf_op jit(solution)/shard_map/ppermute | solution.py:26
  2.0 4.0 %collective-permute-start.4 = (bf16[4,128,128]{2,1,0:T(8,128)(2,1)}, bf16[4,128,128]{2,1,0:T(8,128)(2,1)S(1)}, u32[]{:S(2)}, u32[]{:S(2)}) collective-permute-start(bf16[4,128,128]{2,1,0:T(8,128)(2,1)} %bitcast.8), channel_id=1, source_target_pairs={{0,48},{1,49},{2,50},{3,51},{4,52},{5,53},{6,54},{7,55},{8,56},{9,... | collective-permute-start | bytes 393224 | tf_op jit(solution)/shard_map/ppermute | solution.py:26
  6.0 4.9 %collective-permute-done.4 = bf16[4,128,128]{2,1,0:T(8,128)(2,1)S(1)} collective-permute-done((bf16[4,128,128]{2,1,0:T(8,128)(2,1)}, bf16[4,128,128]{2,1,0:T(8,128)(2,1)S(1)}, u32[]{:S(2)}, u32[]{:S(2)}) %collective-permute-start.4) | collective-permute-done | bytes 131104 | tf_op jit(solution)/shard_map/ppermute | solution.py:26
  11.0 1.7 %collective-permute-start.9 = (bf16[8,128,128]{2,1,0:T(8,128)(2,1)S(1)}, bf16[8,128,128]{2,1,0:T(8,128)(2,1)S(1)}, u32[]{:S(2)}, u32[]{:S(2)}) collective-permute-start(bf16[8,128,128]{2,1,0:T(8,128)(2,1)S(1)} %constant_dynamic-update-slice_fusion.rest_0_), channel_id=1, source_target_pairs={{0,14},{1,3},{2,0},{3,5},{4,2},{5,7},{6,4},{7,9},{8,6},{9,11},{10,... | collective-permute-start | bytes 786440 | tf_op jit(solution)/shard_map/ppermute | solution.py:26
  12.7 2.7 %collective-permute-start.2 = (bf16[4,256,256]{2,1,0:T(8,128)(2,1)}, bf16[4,256,256]{2,1,0:T(8,128)(2,1)S(1)}, u32[]{:S(2)}, u32[]{:S(2)}) collective-permute-start(bf16[4,256,256]{2,1,0:T(8,128)(2,1)} %bitcast.5), channel_id=1, source_target_pairs={{0,64},{1,193},{2,66},{3,195},{4,68},{5,197},{6,70},{7,199},{8,72}... | collective-permute-start | bytes 1572872 | tf_op jit(solution)/shard_map/ppermute | solution.py:26
  15.4 4.1 %collective-permute-start.5 = (bf16[8,128,128]{2,1,0:T(8,128)(2,1)S(1)}, bf16[8,128,128]{2,1,0:T(8,128)(2,1)S(1)}, u32[]{:S(2)}, u32[]{:S(2)}) collective-permute-start(bf16[8,128,128]{2,1,0:T(8,128)(2,1)S(1)} %constant_dynamic-update-slice_fusion.rest_0_), channel_id=1, source_target_pairs={{0,2},{1,15},{2,4},{3,1},{4,6},{5,3},{6,8},{7,5},{8,10},{9,7},{10,... | collective-permute-start | bytes 786440 | tf_op jit(solution)/shard_map/ppermute | solution.py:26
  19.5 2.4 %collective-permute-start.27 = (bf16[8,128,128]{2,1,0:T(8,128)(2,1)S(1)}, bf16[8,128,128]{2,1,0:T(8,128)(2,1)S(1)}, u32[]{:S(2)}, u32[]{:S(2)}) collective-permute-start(bf16[8,128,128]{2,1,0:T(8,128)(2,1)S(1)} %constant_dynamic-update-slice_fusion.rest_0_), channel_id=1, source_target_pairs={{0,48},{1,17},{2,50},{3,19},{4,52},{5,21},{6,54},{7,23},{8,56},{9,... | collective-permute-start | bytes 786440 | tf_op jit(solution)/shard_map/ppermute | solution.py:26
  21.8 2.3 %collective-permute-start.28 = (bf16[8,128,128]{2,1,0:T(8,128)(2,1)S(1)}, bf16[8,128,128]{2,1,0:T(8,128)(2,1)S(1)}, u32[]{:S(2)}, u32[]{:S(2)}) collective-permute-start(bf16[8,128,128]{2,1,0:T(8,128)(2,1)S(1)} %constant_dynamic-update-slice_fusion.rest_0_), channel_id=1, source_target_pairs={{0,1},{1,0},{2,3},{3,2},{4,5},{5,4},{6,7},{7,6},{8,9},{9,8},{10,11... | collective-permute-start | bytes 786440 | tf_op jit(solution)/shard_map/ppermute | solution.py:26
  24.2 4.2 %collective-permute-start.32 = (bf16[8,128,128]{2,1,0:T(8,128)(2,1)S(1)}, bf16[8,128,128]{2,1,0:T(8,128)(2,1)S(1)}, u32[]{:S(2)}, u32[]{:S(2)}) collective-permute-start(bf16[8,128,128]{2,1,0:T(8,128)(2,1)S(1)} %collective-permute-done.9.rest_8_), channel_id=1, source_target_pairs={{0,48},{1,17},{2,50},{3,19},{4,52},{5,21},{6,54},{7,23},{8,56},{9,... | collective-permute-start | bytes 786440 | tf_op jit(solution)/shard_map/ppermute | solution.py:26
  28.4 0.1 collective-permute-start.30
  28.5 3.4 %collective-permute-start.31 = (bf16[8,128,128]{2,1,0:T(8,128)(2,1)S(1)}, bf16[8,128,128]{2,1,0:T(8,128)(2,1)S(1)}, u32[]{:S(2)}, u32[]{:S(2)}) collective-permute-start(bf16[8,128,128]{2,1,0:T(8,128)(2,1)S(1)} %collective-permute-done.9.rest_8_), channel_id=1, source_target_pairs={{0,1},{1,0},{2,3},{3,2},{4,5},{5,4},{6,7},{7,6},{8,9},{9,8},{10,11... | collective-permute-start | bytes 786440 | tf_op jit(solution)/shard_map/ppermute | solution.py:26
  31.9 0.1 collective-permute-start.34
  32.0 0.2 collective-permute-done.32.rest_9_
  32.1 3.2 %collective-permute-start.6 = (bf16[8,128,128]{2,1,0:T(8,128)(2,1)S(1)}, bf16[8,128,128]{2,1,0:T(8,128)(2,1)}, u32[]{:S(2)}, u32[]{:S(2)}) collective-permute-start(bf16[8,128,128]{2,1,0:T(8,128)(2,1)S(1)} %collective-permute-done.5.rest_4_), channel_id=1, source_target_pairs={{0,2},{1,15},{2,4},{3,1},{4,6},{5,3},{6,8},{7,5},{8,10},{9,7},{10,... | collective-permute-start | bytes 786440 | tf_op jit(solution)/shard_map/ppermute | solution.py:26
  35.3 3.6 %collective-permute-start.29 = (bf16[8,128,128]{2,1,0:T(8,128)(2,1)S(1)}, bf16[8,128,128]{2,1,0:T(8,128)(2,1)S(1)}, u32[]{:S(2)}, u32[]{:S(2)}) collective-permute-start(bf16[8,128,128]{2,1,0:T(8,128)(2,1)S(1)} %collective-permute-done.27.rest_1_), channel_id=1, source_target_pairs={{0,1},{1,0},{2,3},{3,2},{4,5},{5,4},{6,7},{7,6},{8,9},{9,8},{10,11... | collective-permute-start | bytes 786440 | tf_op jit(solution)/shard_map/ppermute | solution.py:26
  38.9 0.7 copy-done.1
  39.6 0.7 copy-done.3
  40.3 0.5 collective-permute-start.35
  40.9 1.7 %collective-permute-start.23 = (bf16[8,128,128]{2,1,0:T(8,128)(2,1)}, bf16[8,128,128]{2,1,0:T(8,128)(2,1)}, u32[]{:S(2)}, u32[]{:S(2)}) collective-permute-start(bf16[8,128,128]{2,1,0:T(8,128)(2,1)} %collective-permute-done.10.rest_4_), channel_id=1, source_target_pairs={{0,48},{1,17},{2,50},{3,19},{4,52},{5,21},{6,54},{7,23},{8,56},{9,... | collective-permute-start | bytes 786440 | tf_op jit(solution)/shard_map/ppermute | solution.py:26
  42.7 0.7 copy-done.5
  43.4 0.4 collective-permute-start.1
  43.8 0.7 copy-done.7
  44.4 5.3 %collective-permute-start.22 = (bf16[8,128,128]{2,1,0:T(8,128)(2,1)}, bf16[8,128,128]{2,1,0:T(8,128)(2,1)S(1)}, u32[]{:S(2)}, u32[]{:S(2)}) collective-permute-start(bf16[8,128,128]{2,1,0:T(8,128)(2,1)} %collective-permute-done.10.rest_4_), channel_id=1, source_target_pairs={{0,1},{1,0},{2,3},{3,2},{4,5},{5,4},{6,7},{7,6},{8,9},{9,8},{10,11... | collective-permute-start | bytes 786440 | tf_op jit(solution)/shard_map/ppermute | solution.py:26
  49.8 0.7 copy-done.9
  50.5 0.8 collective-permute-start.7
  51.3 0.7 collective-permute-start.11
  52.0 0.7 copy-done.11
  52.7 3.2 %collective-permute-start.24 = (bf16[8,128,128]{2,1,0:T(8,128)(2,1)}, bf16[8,128,128]{2,1,0:T(8,128)(2,1)}, u32[]{:S(2)}, u32[]{:S(2)}) collective-permute-start(bf16[8,128,128]{2,1,0:T(8,128)(2,1)} %collective-permute-done.23.rest_5_), channel_id=1, source_target_pairs={{0,1},{1,0},{2,3},{3,2},{4,5},{5,4},{6,7},{7,6},{8,9},{9,8},{10,11... | collective-permute-start | bytes 786440 | tf_op jit(solution)/shard_map/ppermute | solution.py:26
  55.9 0.7 copy-done.13
  56.6 1.2 %collective-permute-done.7.rest_0_ = bf16[8,128,128]{2,1,0:T(8,128)(2,1)} collective-permute-done((bf16[8,128,128]{2,1,0:T(8,128)(2,1)}, bf16[8,128,128]{2,1,0:T(8,128)(2,1)}, u32[]{:S(2)}, u32[]{:S(2)}) %collective-permute-start.7) | collective-permute-done | bytes 262176 | tf_op jit(solution)/shard_map/ppermute | solution.py:26
  57.8 3.1 %collective-permute-done.11.rest_4_ = bf16[8,128,128]{2,1,0:T(8,128)(2,1)} collective-permute-done((bf16[8,128,128]{2,1,0:T(8,128)(2,1)}, bf16[8,128,128]{2,1,0:T(8,128)(2,1)}, u32[]{:S(2)}, u32[]{:S(2)}) %collective-permute-start.11) | collective-permute-done | bytes 262176 | tf_op jit(solution)/shard_map/ppermute | solution.py:26
  60.9 0.3 collective-permute-start.17
  61.2 0.2 collective-permute-start.18
  61.4 2.3 %collective-permute-start.15 = (bf16[8,128,128]{2,1,0:T(8,128)(2,1)}, bf16[8,128,128]{2,1,0:T(8,128)(2,1)S(1)}, u32[]{:S(2)}, u32[]{:S(2)}) collective-permute-start(bf16[8,128,128]{2,1,0:T(8,128)(2,1)} %collective-permute-done.7.rest_0_), channel_id=1, source_target_pairs={{0,1},{1,0},{2,3},{3,2},{4,5},{5,4},{6,7},{7,6},{8,9},{9,8},{10,11... | collective-permute-start | bytes 786440 | tf_op jit(solution)/shard_map/ppermute | solution.py:26
  63.8 1.0 %copy-done = bf16[4,1,256,256]{3,2,1,0:T(8,128)(2,1)S(1)} copy-done((bf16[4,1,256,256]{3,2,1,0:T(8,128)(2,1)S(1)}, bf16[4,1,256,256]{3,2,1,0:T(8,128)(2,1)}, u32[]{:S(2)}) %copy-start) | copy-done | bytes 524312
  64.8 0.7 copy-done.15
  65.5 0.7 copy-done.16
  66.1 3.2 %mixed.4 = (bf16[4,16,256,512]{3,2,1,0:T(8,128)(2,1)S(1)}, bf16[256,2048]{1,0:T(8,128)(2,1)S(1)}) custom-call(s32[2]{0:T(128)S(1)} %pad_add_fusion.pos, s32[64]{0:T(128)S(1)} %copy-done.15, s32[64]{0:T(128)S(1)} %copy-done.16, bf16[256,8192]{1,0:T(8,128)(2,1)} %psi_ref.1, bf16[4,256,256]{2,1,0:T(8,128)(2,1)S(1)} %bitcast.6), custom_call_target="tpu_custom_call" | custom-call | flops 1073741824 | bytes 6291456 | tf_op jit(solution)/shard_map/mixed/pallas_call | solution.py:95
  69.4 1.3 %mixed.5.kept = bf16[4,16,256,512]{3,2,1,0:T(8,128)(2,1)S(1)} custom-call(bf16[256,2048]{1,0:T(8,128)(2,1)S(1)} %get-tuple-element.7.masked_ref, bf16[4,256,256]{2,1,0:T(8,128)(2,1)S(1)} %collective-permute-done.left, bf16[4,16,256,512]{3,2,1,0:T(8,128)(2,1)S(1)} %get-tuple-element.8.kept), custom_call_target="tpu_custom_call", output_to_operand_aliasing={{}: (2, {})} | custom-call | flops 1073741824 | bytes 6291456 | tf_op jit(solution)/shard_map/mixed/pallas_call | solution.py:115
  70.6 0.9 %collective-permute-start.12 = (bf16[8,128,128]{2,1,0:T(8,128)(2,1)}, bf16[8,128,128]{2,1,0:T(8,128)(2,1)S(1)}, u32[]{:S(2)}, u32[]{:S(2)}) collective-permute-start(bf16[8,128,128]{2,1,0:T(8,128)(2,1)} %collective-permute-done.11.rest_4_), channel_id=1, source_target_pairs={{0,1},{1,0},{2,3},{3,2},{4,5},{5,4},{6,7},{7,6},{8,9},{9,8},{10,11... | collective-permute-start | bytes 786440 | tf_op jit(solution)/shard_map/ppermute | solution.py:26
  71.5 0.3 collective-permute-start.16
  71.9 1.8 %collective-permute-start.19 = (bf16[8,128,128]{2,1,0:T(8,128)(2,1)S(1)}, bf16[8,128,128]{2,1,0:T(8,128)(2,1)S(1)}, u32[]{:S(2)}, u32[]{:S(2)}) collective-permute-start(bf16[8,128,128]{2,1,0:T(8,128)(2,1)S(1)} %collective-permute-done.17.rest_8_), channel_id=1, source_target_pairs={{0,1},{1,0},{2,3},{3,2},{4,5},{5,4},{6,7},{7,6},{8,9},{9,8},{10,11... | collective-permute-start | bytes 786440 | tf_op jit(solution)/shard_map/ppermute | solution.py:26
  73.7 0.5 collective-permute-start.14
  74.2 1.3 %mixed.6.kept = bf16[4,16,256,512]{3,2,1,0:T(8,128)(2,1)S(1)} custom-call(bf16[256,2048]{1,0:T(8,128)(2,1)S(1)} %get-tuple-element.7.masked_ref, bf16[4,256,256]{2,1,0:T(8,128)(2,1)S(1)} %collective-permute-done.2.left, bf16[4,16,256,512]{3,2,1,0:T(8,128)(2,1)S(1)} %mixed.5.kept), custom_call_target="tpu_custom_call", output_to_operand_aliasing={{}: (2, {})} | custom-call | flops 1073741824 | bytes 6291456 | tf_op jit(solution)/shard_map/mixed/pallas_call | solution.py:115
  75.5 1.3 %mixed.7 = bf16[4,16,256,512]{3,2,1,0:T(8,128)(2,1)S(1)} custom-call(bf16[256,2048]{1,0:T(8,128)(2,1)S(1)} %get-tuple-element.7.masked_ref, bf16[4,256,256]{2,1,0:T(8,128)(2,1)S(1)} %collective-permute-done.1.left, bf16[4,16,256,512]{3,2,1,0:T(8,128)(2,1)S(1)} %mixed.6.kept), custom_call_target="tpu_custom_call", output_to_operand_aliasing={{}: (2, {})} | custom-call | flops 1073741824 | bytes 6291456 | tf_op jit(solution)/shard_map/mixed/pallas_call | solution.py:115
  76.9 3.5 %total.3.rest_8_ = f32[256,2048]{1,0:T(8,128)} custom-call(s32[2]{0:T(128)S(1)} %pad_add_fusion.pos, s32[64]{0:T(128)S(1)} %copy-done.15, s32[64]{0:T(128)S(1)} %copy-done.16, bf16[4,16,256,512]{3,2,1,0:T(8,128)(2,1)S(1)} %mixed.7, bf16[8,128,128]{2,1,0:T(8,128)(2,1)S(1)} %constant_dynamic-update-slice_fusion.rest_0_, ...), custom_call_target="tpu_custom_call" | custom-call | flops 805306368 | bytes 4194304 | tf_op jit(solution)/shard_map/total/pallas_call | solution.py:182
  80.4 4.1 %total.4.rest_12_ = f32[256,2048]{1,0:T(8,128)} custom-call(s32[2]{0:T(128)S(1)} %pad_add_fusion.pos, s32[64]{0:T(128)S(1)} %copy-done.15, s32[64]{0:T(128)S(1)} %copy-done.16, bf16[4,16,256,512]{3,2,1,0:T(8,128)(2,1)S(1)} %mixed.7, bf16[8,128,128]{2,1,0:T(8,128)(2,1)} %collective-permute-done.6.rest_0_, ...), custom_call_target="tpu_custom_call", output_to_operand_aliasing={{}: (12, {})} | custom-call | flops 536870912 | bytes 4194304 | tf_op jit(solution)/shard_map/total/pallas_call | solution.py:182
  84.6 4.6 %total.5 = f32[256,2048]{1,0:T(8,128)} custom-call(s32[2]{0:T(128)S(1)} %pad_add_fusion.pos, s32[64]{0:T(128)S(1)} %copy-done.15, s32[64]{0:T(128)S(1)} %copy-done.16, bf16[4,16,256,512]{3,2,1,0:T(8,128)(2,1)S(1)} %mixed.7, bf16[8,128,128]{2,1,0:T(8,128)(2,1)} %collective-permute-done.7.rest_0_, ...), custom_call_target="tpu_custom_call", output_to_operand_aliasing={{}: (16, {})} | custom-call | flops 805306368 | bytes 4194304 | tf_op jit(solution)/shard_map/total/pallas_call | solution.py:182
  (68 shorter events, 0.4 us)
Async XLA Ops:
  0.0 6.0 %collective-permute-start.3 = (bf16[4,128,128]{2,1,0:T(8,128)(2,1)}, bf16[4,128,128]{2,1,0:T(8,128)(2,1)S(1)}, u32[]{:S(2)}, u32[]{:S(2)}) collective-permute-start(bf16[4,128,128]{2,1,0:T(8,128)(2,1)} %bitcast.7), channel_id=1, source_target_pairs={{0,16},{1,17},{2,18},{3,19},{4,20},{5,21},{6,22},{7,23},{8,24},{9,... | collective-permute-start | bytes 393224 | tf_op jit(solution)/shard_map/ppermute | solution.py:26
  2.0 8.9 %collective-permute-start.4 = (bf16[4,128,128]{2,1,0:T(8,128)(2,1)}, bf16[4,128,128]{2,1,0:T(8,128)(2,1)S(1)}, u32[]{:S(2)}, u32[]{:S(2)}) collective-permute-start(bf16[4,128,128]{2,1,0:T(8,128)(2,1)} %bitcast.8), channel_id=1, source_target_pairs={{0,48},{1,49},{2,50},{3,51},{4,52},{5,53},{6,54},{7,55},{8,56},{9,... | collective-permute-start | bytes 393224 | tf_op jit(solution)/shard_map/ppermute | solution.py:26
  11.0 10.9 %collective-permute-start.9 = (bf16[8,128,128]{2,1,0:T(8,128)(2,1)S(1)}, bf16[8,128,128]{2,1,0:T(8,128)(2,1)S(1)}, u32[]{:S(2)}, u32[]{:S(2)}) collective-permute-start(bf16[8,128,128]{2,1,0:T(8,128)(2,1)S(1)} %constant_dynamic-update-slice_fusion.rest_0_), channel_id=1, source_target_pairs={{0,14},{1,3},{2,0},{3,5},{4,2},{5,7},{6,4},{7,9},{8,6},{9,11},{10,... | collective-permute-start | bytes 786440 | tf_op jit(solution)/shard_map/ppermute | solution.py:26
  12.7 19.2 %collective-permute-start = (bf16[4,256,256]{2,1,0:T(8,128)(2,1)}, bf16[4,256,256]{2,1,0:T(8,128)(2,1)S(1)}, u32[]{:S(2)}, u32[]{:S(2)}) collective-permute-start(bf16[4,256,256]{2,1,0:T(8,128)(2,1)} %bitcast.4), channel_id=1, source_target_pairs={{0,192},{1,65},{2,194},{3,67},{4,196},{5,69},{6,198},{7,71},{8,200... | collective-permute-start | bytes 1572872 | tf_op jit(solution)/shard_map/ppermute | solution.py:26
  12.7 19.3 %collective-permute-start.2 = (bf16[4,256,256]{2,1,0:T(8,128)(2,1)}, bf16[4,256,256]{2,1,0:T(8,128)(2,1)S(1)}, u32[]{:S(2)}, u32[]{:S(2)}) collective-permute-start(bf16[4,256,256]{2,1,0:T(8,128)(2,1)} %bitcast.5), channel_id=1, source_target_pairs={{0,64},{1,193},{2,66},{3,195},{4,68},{5,197},{6,70},{7,199},{8,72}... | collective-permute-start | bytes 1572872 | tf_op jit(solution)/shard_map/ppermute | solution.py:26
  15.4 8.8 %collective-permute-start.5 = (bf16[8,128,128]{2,1,0:T(8,128)(2,1)S(1)}, bf16[8,128,128]{2,1,0:T(8,128)(2,1)S(1)}, u32[]{:S(2)}, u32[]{:S(2)}) collective-permute-start(bf16[8,128,128]{2,1,0:T(8,128)(2,1)S(1)} %constant_dynamic-update-slice_fusion.rest_0_), channel_id=1, source_target_pairs={{0,2},{1,15},{2,4},{3,1},{4,6},{5,3},{6,8},{7,5},{8,10},{9,7},{10,... | collective-permute-start | bytes 786440 | tf_op jit(solution)/shard_map/ppermute | solution.py:26
  19.5 8.9 %collective-permute-start.27 = (bf16[8,128,128]{2,1,0:T(8,128)(2,1)S(1)}, bf16[8,128,128]{2,1,0:T(8,128)(2,1)S(1)}, u32[]{:S(2)}, u32[]{:S(2)}) collective-permute-start(bf16[8,128,128]{2,1,0:T(8,128)(2,1)S(1)} %constant_dynamic-update-slice_fusion.rest_0_), channel_id=1, source_target_pairs={{0,48},{1,17},{2,50},{3,19},{4,52},{5,21},{6,54},{7,23},{8,56},{9,... | collective-permute-start | bytes 786440 | tf_op jit(solution)/shard_map/ppermute | solution.py:26
  21.8 6.6 %collective-permute-start.28 = (bf16[8,128,128]{2,1,0:T(8,128)(2,1)S(1)}, bf16[8,128,128]{2,1,0:T(8,128)(2,1)S(1)}, u32[]{:S(2)}, u32[]{:S(2)}) collective-permute-start(bf16[8,128,128]{2,1,0:T(8,128)(2,1)S(1)} %constant_dynamic-update-slice_fusion.rest_0_), channel_id=1, source_target_pairs={{0,1},{1,0},{2,3},{3,2},{4,5},{5,4},{6,7},{7,6},{8,9},{9,8},{10,11... | collective-permute-start | bytes 786440 | tf_op jit(solution)/shard_map/ppermute | solution.py:26
  24.2 8.0 %collective-permute-start.32 = (bf16[8,128,128]{2,1,0:T(8,128)(2,1)S(1)}, bf16[8,128,128]{2,1,0:T(8,128)(2,1)S(1)}, u32[]{:S(2)}, u32[]{:S(2)}) collective-permute-start(bf16[8,128,128]{2,1,0:T(8,128)(2,1)S(1)} %collective-permute-done.9.rest_8_), channel_id=1, source_target_pairs={{0,48},{1,17},{2,50},{3,19},{4,52},{5,21},{6,54},{7,23},{8,56},{9,... | collective-permute-start | bytes 786440 | tf_op jit(solution)/shard_map/ppermute | solution.py:26
  28.4 7.0 %collective-permute-start.30 = (bf16[8,128,128]{2,1,0:T(8,128)(2,1)S(1)}, bf16[8,128,128]{2,1,0:T(8,128)(2,1)S(1)}, u32[]{:S(2)}, u32[]{:S(2)}) collective-permute-start(bf16[8,128,128]{2,1,0:T(8,128)(2,1)S(1)} %collective-permute-done.5.rest_4_), channel_id=1, source_target_pairs={{0,48},{1,17},{2,50},{3,19},{4,52},{5,21},{6,54},{7,23},{8,56},{9,... | collective-permute-start | bytes 786440 | tf_op jit(solution)/shard_map/ppermute | solution.py:26
  28.5 10.5 %collective-permute-start.31 = (bf16[8,128,128]{2,1,0:T(8,128)(2,1)S(1)}, bf16[8,128,128]{2,1,0:T(8,128)(2,1)S(1)}, u32[]{:S(2)}, u32[]{:S(2)}) collective-permute-start(bf16[8,128,128]{2,1,0:T(8,128)(2,1)S(1)} %collective-permute-done.9.rest_8_), channel_id=1, source_target_pairs={{0,1},{1,0},{2,3},{3,2},{4,5},{5,4},{6,7},{7,6},{8,9},{9,8},{10,11... | collective-permute-start | bytes 786440 | tf_op jit(solution)/shard_map/ppermute | solution.py:26
  31.9 7.8 %collective-permute-start.34 = (bf16[8,128,128]{2,1,0:T(8,128)(2,1)S(1)}, bf16[8,128,128]{2,1,0:T(8,128)(2,1)S(1)}, u32[]{:S(2)}, u32[]{:S(2)}) collective-permute-start(bf16[8,128,128]{2,1,0:T(8,128)(2,1)S(1)} %collective-permute-done.5.rest_4_), channel_id=1, source_target_pairs={{0,1},{1,0},{2,3},{3,2},{4,5},{5,4},{6,7},{7,6},{8,9},{9,8},{10,11... | collective-permute-start | bytes 786440 | tf_op jit(solution)/shard_map/ppermute | solution.py:26
  32.0 8.9 %collective-permute-start.10 = (bf16[8,128,128]{2,1,0:T(8,128)(2,1)S(1)}, bf16[8,128,128]{2,1,0:T(8,128)(2,1)}, u32[]{:S(2)}, u32[]{:S(2)}) collective-permute-start(bf16[8,128,128]{2,1,0:T(8,128)(2,1)S(1)} %collective-permute-done.9.rest_8_), channel_id=1, source_target_pairs={{0,14},{1,3},{2,0},{3,5},{4,2},{5,7},{6,4},{7,9},{8,6},{9,11},{10,... | collective-permute-start | bytes 786440 | tf_op jit(solution)/shard_map/ppermute | solution.py:26
  32.1 10.5 %collective-permute-start.6 = (bf16[8,128,128]{2,1,0:T(8,128)(2,1)S(1)}, bf16[8,128,128]{2,1,0:T(8,128)(2,1)}, u32[]{:S(2)}, u32[]{:S(2)}) collective-permute-start(bf16[8,128,128]{2,1,0:T(8,128)(2,1)S(1)} %collective-permute-done.5.rest_4_), channel_id=1, source_target_pairs={{0,2},{1,15},{2,4},{3,1},{4,6},{5,3},{6,8},{7,5},{8,10},{9,7},{10,... | collective-permute-start | bytes 786440 | tf_op jit(solution)/shard_map/ppermute | solution.py:26
  35.3 7.3 %collective-permute-start.29 = (bf16[8,128,128]{2,1,0:T(8,128)(2,1)S(1)}, bf16[8,128,128]{2,1,0:T(8,128)(2,1)S(1)}, u32[]{:S(2)}, u32[]{:S(2)}) collective-permute-start(bf16[8,128,128]{2,1,0:T(8,128)(2,1)S(1)} %collective-permute-done.27.rest_1_), channel_id=1, source_target_pairs={{0,1},{1,0},{2,3},{3,2},{4,5},{5,4},{6,7},{7,6},{8,9},{9,8},{10,11... | collective-permute-start | bytes 786440 | tf_op jit(solution)/shard_map/ppermute | solution.py:26
  38.9 0.7 copy-start.1
  39.6 4.1 %collective-permute-start.33 = (bf16[8,128,128]{2,1,0:T(8,128)(2,1)S(1)}, bf16[8,128,128]{2,1,0:T(8,128)(2,1)S(1)}, u32[]{:S(2)}, u32[]{:S(2)}) collective-permute-start(bf16[8,128,128]{2,1,0:T(8,128)(2,1)S(1)} %collective-permute-done.32.rest_9_), channel_id=1, source_target_pairs={{0,1},{1,0},{2,3},{3,2},{4,5},{5,4},{6,7},{7,6},{8,9},{9,8},{10,11... | collective-permute-start | bytes 786440 | tf_op jit(solution)/shard_map/ppermute | solution.py:26
  39.6 0.7 copy-start.3
  40.3 9.4 %collective-permute-start.35 = (bf16[8,128,128]{2,1,0:T(8,128)(2,1)S(1)}, bf16[8,128,128]{2,1,0:T(8,128)(2,1)S(1)}, u32[]{:S(2)}, u32[]{:S(2)}) collective-permute-start(bf16[8,128,128]{2,1,0:T(8,128)(2,1)S(1)} %collective-permute-done.30.rest_5_), channel_id=1, source_target_pairs={{0,1},{1,0},{2,3},{3,2},{4,5},{5,4},{6,7},{7,6},{8,9},{9,8},{10,11... | collective-permute-start | bytes 786440 | tf_op jit(solution)/shard_map/ppermute | solution.py:26
  40.9 9.6 %collective-permute-start.23 = (bf16[8,128,128]{2,1,0:T(8,128)(2,1)}, bf16[8,128,128]{2,1,0:T(8,128)(2,1)}, u32[]{:S(2)}, u32[]{:S(2)}) collective-permute-start(bf16[8,128,128]{2,1,0:T(8,128)(2,1)} %collective-permute-done.10.rest_4_), channel_id=1, source_target_pairs={{0,48},{1,17},{2,50},{3,19},{4,52},{5,21},{6,54},{7,23},{8,56},{9,... | collective-permute-start | bytes 786440 | tf_op jit(solution)/shard_map/ppermute | solution.py:26
  42.6 8.7 %collective-permute-start.21 = (bf16[8,128,128]{2,1,0:T(8,128)(2,1)}, bf16[8,128,128]{2,1,0:T(8,128)(2,1)}, u32[]{:S(2)}, u32[]{:S(2)}) collective-permute-start(bf16[8,128,128]{2,1,0:T(8,128)(2,1)} %collective-permute-done.6.rest_0_), channel_id=1, source_target_pairs={{0,48},{1,17},{2,50},{3,19},{4,52},{5,21},{6,54},{7,23},{8,56},{9,... | collective-permute-start | bytes 786440 | tf_op jit(solution)/shard_map/ppermute | solution.py:26
  42.7 0.7 copy-start.5
  43.4 17.9 %collective-permute-start.1 = (bf16[4,256,256]{2,1,0:T(8,128)(2,1)S(1)}, bf16[4,256,256]{2,1,0:T(8,128)(2,1)S(1)}, u32[]{:S(2)}, u32[]{:S(2)}) collective-permute-start(bf16[4,256,256]{2,1,0:T(8,128)(2,1)S(1)} %collective-permute-done.left), channel_id=1, source_target_pairs={{0,192},{1,65},{2,194},{3,67},{4,196},{5,69},{6,198},{7,71},{8,200... | collective-permute-start | bytes 1572872 | tf_op jit(solution)/shard_map/ppermute | solution.py:26
  44.4 7.5 %collective-permute-start.22 = (bf16[8,128,128]{2,1,0:T(8,128)(2,1)}, bf16[8,128,128]{2,1,0:T(8,128)(2,1)S(1)}, u32[]{:S(2)}, u32[]{:S(2)}) collective-permute-start(bf16[8,128,128]{2,1,0:T(8,128)(2,1)} %collective-permute-done.10.rest_4_), channel_id=1, source_target_pairs={{0,1},{1,0},{2,3},{3,2},{4,5},{5,4},{6,7},{7,6},{8,9},{9,8},{10,11... | collective-permute-start | bytes 786440 | tf_op jit(solution)/shard_map/ppermute | solution.py:26
  50.5 5.4 %collective-permute-start.25 = (bf16[8,128,128]{2,1,0:T(8,128)(2,1)}, bf16[8,128,128]{2,1,0:T(8,128)(2,1)S(1)}, u32[]{:S(2)}, u32[]{:S(2)}) collective-permute-start(bf16[8,128,128]{2,1,0:T(8,128)(2,1)} %collective-permute-done.6.rest_0_), channel_id=1, source_target_pairs={{0,1},{1,0},{2,3},{3,2},{4,5},{5,4},{6,7},{7,6},{8,9},{9,8},{10,11... | collective-permute-start | bytes 786440 | tf_op jit(solution)/shard_map/ppermute | solution.py:26
  50.5 7.3 %collective-permute-start.7 = (bf16[8,128,128]{2,1,0:T(8,128)(2,1)}, bf16[8,128,128]{2,1,0:T(8,128)(2,1)}, u32[]{:S(2)}, u32[]{:S(2)}) collective-permute-start(bf16[8,128,128]{2,1,0:T(8,128)(2,1)} %collective-permute-done.6.rest_0_), channel_id=1, source_target_pairs={{0,2},{1,15},{2,4},{3,1},{4,6},{5,3},{6,8},{7,5},{8,10},{9,7},{10,... | collective-permute-start | bytes 786440 | tf_op jit(solution)/shard_map/ppermute | solution.py:26
  51.3 9.7 %collective-permute-start.11 = (bf16[8,128,128]{2,1,0:T(8,128)(2,1)}, bf16[8,128,128]{2,1,0:T(8,128)(2,1)}, u32[]{:S(2)}, u32[]{:S(2)}) collective-permute-start(bf16[8,128,128]{2,1,0:T(8,128)(2,1)} %collective-permute-done.10.rest_4_), channel_id=1, source_target_pairs={{0,14},{1,3},{2,0},{3,5},{4,2},{5,7},{6,4},{7,9},{8,6},{9,11},{10,... | collective-permute-start | bytes 786440 | tf_op jit(solution)/shard_map/ppermute | solution.py:26
  52.0 0.7 copy-start.11
  52.7 8.8 %collective-permute-start.24 = (bf16[8,128,128]{2,1,0:T(8,128)(2,1)}, bf16[8,128,128]{2,1,0:T(8,128)(2,1)}, u32[]{:S(2)}, u32[]{:S(2)}) collective-permute-start(bf16[8,128,128]{2,1,0:T(8,128)(2,1)} %collective-permute-done.23.rest_5_), channel_id=1, source_target_pairs={{0,1},{1,0},{2,3},{3,2},{4,5},{5,4},{6,7},{7,6},{8,9},{9,8},{10,11... | collective-permute-start | bytes 786440 | tf_op jit(solution)/shard_map/ppermute | solution.py:26
  56.6 7.1 %collective-permute-start.26 = (bf16[8,128,128]{2,1,0:T(8,128)(2,1)}, bf16[8,128,128]{2,1,0:T(8,128)(2,1)}, u32[]{:S(2)}, u32[]{:S(2)}) collective-permute-start(bf16[8,128,128]{2,1,0:T(8,128)(2,1)} %collective-permute-done.21.rest_1_), channel_id=1, source_target_pairs={{0,1},{1,0},{2,3},{3,2},{4,5},{5,4},{6,7},{7,6},{8,9},{9,8},{10,11... | collective-permute-start | bytes 786440 | tf_op jit(solution)/shard_map/ppermute | solution.py:26
  57.8 12.8 %collective-permute-start.8 = (bf16[8,128,128]{2,1,0:T(8,128)(2,1)}, bf16[8,128,128]{2,1,0:T(8,128)(2,1)S(1)}, u32[]{:S(2)}, u32[]{:S(2)}) collective-permute-start(bf16[8,128,128]{2,1,0:T(8,128)(2,1)} %collective-permute-done.7.rest_0_), channel_id=1, source_target_pairs={{0,48},{1,17},{2,50},{3,19},{4,52},{5,21},{6,54},{7,23},{8,56},{9,... | collective-permute-start | bytes 786440 | tf_op jit(solution)/shard_map/ppermute | solution.py:26
  60.9 10.6 %collective-permute-start.17 = (bf16[8,128,128]{2,1,0:T(8,128)(2,1)}, bf16[8,128,128]{2,1,0:T(8,128)(2,1)S(1)}, u32[]{:S(2)}, u32[]{:S(2)}) collective-permute-start(bf16[8,128,128]{2,1,0:T(8,128)(2,1)} %collective-permute-done.7.rest_0_), channel_id=1, source_target_pairs={{0,2},{1,15},{2,4},{3,1},{4,6},{5,3},{6,8},{7,5},{8,10},{9,7},{10,... | collective-permute-start | bytes 786440 | tf_op jit(solution)/shard_map/ppermute | solution.py:26
  61.2 10.6 %collective-permute-start.18 = (bf16[8,128,128]{2,1,0:T(8,128)(2,1)}, bf16[8,128,128]{2,1,0:T(8,128)(2,1)S(1)}, u32[]{:S(2)}, u32[]{:S(2)}) collective-permute-start(bf16[8,128,128]{2,1,0:T(8,128)(2,1)} %collective-permute-done.7.rest_0_), channel_id=1, source_target_pairs={{0,50},{1,31},{2,52},{3,17},{4,54},{5,19},{6,56},{7,21},{8,58},{9,... | collective-permute-start | bytes 786440 | tf_op jit(solution)/shard_map/ppermute | solution.py:26
  61.4 12.3 %collective-permute-start.15 = (bf16[8,128,128]{2,1,0:T(8,128)(2,1)}, bf16[8,128,128]{2,1,0:T(8,128)(2,1)S(1)}, u32[]{:S(2)}, u32[]{:S(2)}) collective-permute-start(bf16[8,128,128]{2,1,0:T(8,128)(2,1)} %collective-permute-done.7.rest_0_), channel_id=1, source_target_pairs={{0,1},{1,0},{2,3},{3,2},{4,5},{5,4},{6,7},{7,6},{8,9},{9,8},{10,11... | collective-permute-start | bytes 786440 | tf_op jit(solution)/shard_map/ppermute | solution.py:26
  63.7 10.0 %collective-permute-start.13 = (bf16[8,128,128]{2,1,0:T(8,128)(2,1)}, bf16[8,128,128]{2,1,0:T(8,128)(2,1)S(1)}, u32[]{:S(2)}, u32[]{:S(2)}) collective-permute-start(bf16[8,128,128]{2,1,0:T(8,128)(2,1)} %collective-permute-done.11.rest_4_), channel_id=1, source_target_pairs={{0,48},{1,17},{2,50},{3,19},{4,52},{5,21},{6,54},{7,23},{8,56},{9,... | collective-permute-start | bytes 786440 | tf_op jit(solution)/shard_map/ppermute | solution.py:26
  63.8 1.0 %copy-start = (bf16[4,1,256,256]{3,2,1,0:T(8,128)(2,1)S(1)}, bf16[4,1,256,256]{3,2,1,0:T(8,128)(2,1)}, u32[]{:S(2)}) copy-start(bf16[4,1,256,256]{3,2,1,0:T(8,128)(2,1)} %param.6) | copy-start | bytes 1572868
  70.6 13.9 %collective-permute-start.12 = (bf16[8,128,128]{2,1,0:T(8,128)(2,1)}, bf16[8,128,128]{2,1,0:T(8,128)(2,1)S(1)}, u32[]{:S(2)}, u32[]{:S(2)}) collective-permute-start(bf16[8,128,128]{2,1,0:T(8,128)(2,1)} %collective-permute-done.11.rest_4_), channel_id=1, source_target_pairs={{0,1},{1,0},{2,3},{3,2},{4,5},{5,4},{6,7},{7,6},{8,9},{9,8},{10,11... | collective-permute-start | bytes 786440 | tf_op jit(solution)/shard_map/ppermute | solution.py:26
  71.5 13.0 %collective-permute-start.16 = (bf16[8,128,128]{2,1,0:T(8,128)(2,1)S(1)}, bf16[8,128,128]{2,1,0:T(8,128)(2,1)S(1)}, u32[]{:S(2)}, u32[]{:S(2)}) collective-permute-start(bf16[8,128,128]{2,1,0:T(8,128)(2,1)S(1)} %collective-permute-done.8.rest_1_), channel_id=1, source_target_pairs={{0,1},{1,0},{2,3},{3,2},{4,5},{5,4},{6,7},{7,6},{8,9},{9,8},{10,11... | collective-permute-start | bytes 786440 | tf_op jit(solution)/shard_map/ppermute | solution.py:26
  71.9 12.7 %collective-permute-start.19 = (bf16[8,128,128]{2,1,0:T(8,128)(2,1)S(1)}, bf16[8,128,128]{2,1,0:T(8,128)(2,1)S(1)}, u32[]{:S(2)}, u32[]{:S(2)}) collective-permute-start(bf16[8,128,128]{2,1,0:T(8,128)(2,1)S(1)} %collective-permute-done.17.rest_8_), channel_id=1, source_target_pairs={{0,1},{1,0},{2,3},{3,2},{4,5},{5,4},{6,7},{7,6},{8,9},{9,8},{10,11... | collective-permute-start | bytes 786440 | tf_op jit(solution)/shard_map/ppermute | solution.py:26
  73.7 10.9 %collective-permute-start.20 = (bf16[8,128,128]{2,1,0:T(8,128)(2,1)S(1)}, bf16[8,128,128]{2,1,0:T(8,128)(2,1)S(1)}, u32[]{:S(2)}, u32[]{:S(2)}) collective-permute-start(bf16[8,128,128]{2,1,0:T(8,128)(2,1)S(1)} %collective-permute-done.18.rest_9_), channel_id=1, source_target_pairs={{0,1},{1,0},{2,3},{3,2},{4,5},{5,4},{6,7},{7,6},{8,9},{9,8},{10,11... | collective-permute-start | bytes 786440 | tf_op jit(solution)/shard_map/ppermute | solution.py:26
  73.7 10.9 %collective-permute-start.14 = (bf16[8,128,128]{2,1,0:T(8,128)(2,1)S(1)}, bf16[8,128,128]{2,1,0:T(8,128)(2,1)S(1)}, u32[]{:S(2)}, u32[]{:S(2)}) collective-permute-start(bf16[8,128,128]{2,1,0:T(8,128)(2,1)S(1)} %collective-permute-done.13.rest_5_), channel_id=1, source_target_pairs={{0,1},{1,0},{2,3},{3,2},{4,5},{5,4},{6,7},{7,6},{8,9},{9,8},{10,11... | collective-permute-start | bytes 786440 | tf_op jit(solution)/shard_map/ppermute | solution.py:26
  75.5 1.3 %copy-start.2 = (bf16[8,128,128]{2,1,0:T(8,128)(2,1)S(1)}, bf16[8,128,128]{2,1,0:T(8,128)(2,1)}, u32[]{:S(2)}) copy-start(bf16[8,128,128]{2,1,0:T(8,128)(2,1)} %copy-done.1) | copy-start | bytes 786436
  75.5 1.3 %copy-start.4 = (bf16[8,128,128]{2,1,0:T(8,128)(2,1)S(1)}, bf16[8,128,128]{2,1,0:T(8,128)(2,1)}, u32[]{:S(2)}) copy-start(bf16[8,128,128]{2,1,0:T(8,128)(2,1)} %copy-done.3) | copy-start | bytes 786436
  75.5 1.3 %copy-start.6 = (bf16[8,128,128]{2,1,0:T(8,128)(2,1)S(1)}, bf16[8,128,128]{2,1,0:T(8,128)(2,1)}, u32[]{:S(2)}) copy-start(bf16[8,128,128]{2,1,0:T(8,128)(2,1)} %copy-done.5) | copy-start | bytes 786436
  75.5 1.3 %copy-start.8 = (bf16[8,128,128]{2,1,0:T(8,128)(2,1)S(1)}, bf16[8,128,128]{2,1,0:T(8,128)(2,1)}, u32[]{:S(2)}) copy-start(bf16[8,128,128]{2,1,0:T(8,128)(2,1)} %copy-done.7) | copy-start | bytes 786436
  75.5 1.3 %copy-start.10 = (bf16[8,128,128]{2,1,0:T(8,128)(2,1)S(1)}, bf16[8,128,128]{2,1,0:T(8,128)(2,1)}, u32[]{:S(2)}) copy-start(bf16[8,128,128]{2,1,0:T(8,128)(2,1)} %copy-done.9) | copy-start | bytes 786436
  76.8 3.6 %copy-start.12 = (bf16[8,128,128]{2,1,0:T(8,128)(2,1)S(1)}, bf16[8,128,128]{2,1,0:T(8,128)(2,1)}, u32[]{:S(2)}) copy-start(bf16[8,128,128]{2,1,0:T(8,128)(2,1)} %copy-done.11) | copy-start | bytes 786436
  76.8 3.6 %copy-start.14 = (bf16[8,128,128]{2,1,0:T(8,128)(2,1)S(1)}, bf16[8,128,128]{2,1,0:T(8,128)(2,1)}, u32[]{:S(2)}) copy-start(bf16[8,128,128]{2,1,0:T(8,128)(2,1)} %copy-done.13) | copy-start | bytes 786436
  (5 other events, 3.4 us)
